TPU v7x, 32 devices: a whole 2x2x4 slice. The times are simulated.
32 devices in a mesh: row: 4 (over z), col: 8 (over y, x, core).
Axes of the slice: x: 2, y: 2, z: 4, core: 2. Of those that a mesh axis runs over, the one named last changes fastest.
Arguments:
- cotangent: float32 [4096, 8192], P('row', 'col'), may hold values from -6 to 6
- whitened: float32 [4096, 8192], P('row', 'col'), may hold values from -0.0625 to 0.0625
- panel_rows: float32 [4, 256, 4096], P(None, None, 'row'), may hold values from -0.375 to 0.375
- diag_inverse: float32 [4, 256, 256], replicated, as said below
Outputs:
- adjoint_rhs: float32 [4096, 8192], P('row', 'col')
- factor_grad: float32 [4, 256, 4096], P(None, 'col', 'row')
Inputs may be any that keep to these rules, and one draw needn't show every extreme that they name: `diag_inverse`: each block is lower triangular with diagonal entries between 0.5 and 1.5.
All inputs are finite; a program needn't handle non-finite values.
Results may differ from a plain program's by a relative error of at most 0.00017.
Values sent between devices are 32-bit elements; how exact they have to be, the bound alone decides.
A program may use at most 128 MiB of HBM per device.

v0:
```python
import functools

import jax
import jax.numpy as jnp
from jax import lax
from jax.experimental import pallas as pl
from jax.experimental.pallas import tpu as pltpu
from jax.sharding import PartitionSpec as P

MESH = pl.DeviceIdType.MESH
CHUNK = 128
HALVES = 2
F32 = jnp.float32
BF16 = jnp.bfloat16


def split(x):
    hi = x.astype(BF16)
    return hi, (x - hi.astype(F32)).astype(BF16)


def product(a, b, dims):
    dot = functools.partial(lax.dot_general, dimension_numbers=(dims, ((), ())), preferred_element_type=F32)
    return dot(a[0], b[0]) + (dot(a[0], b[1]) + dot(a[1], b[0]))


NN = ((1,), (0,))
NT = ((1,), (1,))


def kernel(
    n_row, n_col, cot_hbm, wht_hbm, pan_hbm, diag_hbm, res_ref, out_ref,
    wht_ref, pan_ref, diag_ref, y, pth, ptl, dth, dtl, wh, wl, grad, rs_a, rs_b, far_pan, far_own, far_sum, fph, fpl,
    local_sem, recv_sem, down_sem, up_sem, a_send, a_recv, b_send, b_recv, fp_send, fp_recv, fo_send, fo_recv,
):
    rows, rhs = res_ref.shape
    panels, width = diag_ref.shape[0], diag_ref.shape[1]
    count = rhs // CHUNK
    blocks = rows // width
    tail = rows - width
    part = width // n_col
    chips = n_col // 2
    half = width // HALVES
    row, col = lax.axis_index("row"), lax.axis_index("col")
    core, chip = lax.rem(col, 2), col // 2
    last = panels - 1
    last_root = n_row - panels
    helper = last_root + 1

    def y_copy(p, c, h, sems, step):
        block = y.at[p, c, h * half : (h + 1) * half]
        return pltpu.make_async_remote_copy(
            src_ref=block, dst_ref=block, send_sem=sems.at[p, c, h], recv_sem=recv_sem.at[p, c, h],
            device_id={"row": lax.rem(row + step, n_row)}, device_id_type=MESH,
        )

    def down(p, c, h):
        return y_copy(p, c, h, down_sem, n_row - 1)

    def up(p, c, h):
        return y_copy(p, c, h, up_sem, 1)

    def far_panel(p):
        return pltpu.make_async_remote_copy(
            src_ref=pan_hbm.at[p, :, tail:], dst_ref=far_pan.at[p], send_sem=fp_send.at[p], recv_sem=fp_recv.at[p],
            device_id={"row": lax.rem(row + 1, n_row)}, device_id_type=MESH,
        )

    def far_rows(c):
        return pltpu.make_async_remote_copy(
            src_ref=cot_hbm.at[tail:, columns(c)], dst_ref=far_own.at[c], send_sem=fo_send.at[c], recv_sem=fo_recv.at[c],
            device_id={"row": lax.rem(row + 1, n_row)}, device_id_type=MESH,
        )

    def group(g):
        return slice(0, blocks - 1) if g == 0 else slice(blocks - 1, blocks)

    def pair_copy(p, m, g):
        place = (2 * m + 1 - core) * part
        return pltpu.make_async_remote_copy(
            src_ref=grad.at[p, group(g), pl.ds(pl.multiple_of(place, part), part)], dst_ref=rs_a.at[p, m, group(g)],
            send_sem=a_send.at[p, m, g], recv_sem=a_recv.at[p, m, g],
            device_id={"col": 2 * chip + 1 - core}, device_id_type=MESH,
        )

    def chip_copy(p, j, g):
        peer = lax.rem(chip + j, chips)
        return pltpu.make_async_remote_copy(
            src_ref=rs_a.at[p, peer, group(g)], dst_ref=rs_b.at[p, j, group(g)],
            send_sem=b_send.at[p, j, g], recv_sem=b_recv.at[p, j, g],
            device_id={"col": 2 * peer + core}, device_id_type=MESH,
        )

    def groups(p, act):
        act(0)

        @pl.when(row <= n_row - 1 - p)
        def _():
            act(1)

    def pair_start(p):
        def act(g):
            for m in range(chips):
                pair_copy(p, m, g).start()

        groups(p, act)

    def chip_start(p):
        def act(g):
            for m in range(chips):
                pair_copy(p, m, g).wait_recv()
            for m in range(chips):
                place = pl.multiple_of((2 * m + core) * part, part)
                rs_a[p, m, group(g)] += grad[p, group(g), pl.ds(place, part)]
            for j in range(1, chips):
                chip_copy(p, j, g).start()

        groups(p, act)

    def finish(p):
        def act(g):
            for j in range(1, chips):
                chip_copy(p, j, g).wait_recv()
            for b in range(blocks)[group(g)]:
                total = rs_a[p, chip, b]
                for j in range(1, chips):
                    total = total + rs_b[p, j, b]
                out_ref[p, :, b * width : (b + 1) * width] = total

        out_ref[p, :, tail:] = jnp.zeros((part, width), F32)
        groups(p, act)

    def columns(c):
        return pl.ds(pl.multiple_of(c * CHUNK, CHUNK), CHUNK)

    def solve(p, c, own):
        y[p, c] = product((dth[p], dtl[p]), split(own), NN)

    barrier = pltpu.get_barrier_semaphore()
    for step in (1, n_row - 1):
        pl.semaphore_signal(barrier, inc=1, device_id={"row": lax.rem(row + step, n_row)}, device_id_type=MESH)
    for step in range(1, n_col):
        pl.semaphore_signal(barrier, inc=1, device_id={"col": lax.rem(col + step, n_col)}, device_id_type=MESH)

    diag_copy = pltpu.make_async_copy(diag_hbm, diag_ref, local_sem.at[0])
    tail_copy = pltpu.make_async_copy(cot_hbm.at[tail:], res_ref.at[tail:], local_sem.at[1])
    pan_copy = pltpu.make_async_copy(pan_hbm, pan_ref, local_sem.at[2])
    head_copy = pltpu.make_async_copy(cot_hbm.at[:tail], res_ref.at[:tail], local_sem.at[3])
    wht_copy = pltpu.make_async_copy(wht_hbm, wht_ref, local_sem.at[4])
    def inverse(p):
        hi, lo = split(diag_ref[p].T)
        dth[p] = hi
        dtl[p] = lo

    diag_copy.start()
    tail_copy.start()
    diag_copy.wait()
    inverse(0)
    tail_copy.wait()
    pl.semaphore_wait(barrier, 2 + n_col - 1)

    @pl.when(row == n_row - 1)
    def _():
        @pl.loop(0, count)
        def _(c):
            solve(0, c, res_ref[tail:, columns(c)])
            for h in range(HALVES):
                down(0, c, h).start()

    @pl.when(row == last_root)
    def _():
        @pl.loop(0, last)
        def _(p):
            far_panel(p).start()

        @pl.loop(0, count)
        def _(c):
            far_rows(c).start()

    for copy in (pan_copy, wht_copy, head_copy):
        copy.start()

    @pl.loop(1, panels)
    def _(p):
        inverse(p)

    pan_copy.wait()

    @pl.loop(0, panels)
    def _(p):
        for b in range(blocks):
            hi, lo = split(pan_ref[p, :, b * width : (b + 1) * width].T)
            pth[p, b * width : (b + 1) * width] = hi
            ptl[p, b * width : (b + 1) * width] = lo
        grad[p] = jnp.zeros(grad.shape[1:], F32)

    head_copy.wait()
    wht_copy.wait()

    @pl.loop(0, count)
    def _(c):
        hi, lo = split(wht_ref[:, columns(c)])
        wh[c] = hi
        wl[c] = lo

    far_sum[...] = jnp.zeros(far_sum.shape, F32)

    @pl.loop(0, panels)
    def _(p):
        root = n_row - 1 - p

        @pl.when((row == helper) & (p < last))
        def _():
            far_panel(p).wait_recv()
            hi, lo = split(far_pan[p].T)
            fph[...] = hi
            fpl[...] = lo

        @pl.loop(0, count)
        def _(c):
            for h in range(HALVES):
                @pl.when((row != root) & ((p < last) | (row != helper)))
                def _():
                    down(p, c, h).wait_recv()

                @pl.when((row > root) & (row < n_row - 1) & ((p < last) | (row != helper)))
                def _():
                    up(p, c, h).start()

                @pl.when((row > 0) & ((row < root) | ((row == root) & (p > 0))))
                def _():
                    down(p, c, h).start()

            ys = split(y[p, c])

            @pl.when(row < root)
            def _():
                res_ref[tail:, columns(c)] -= product((pth[p, tail:], ptl[p, tail:]), ys, NN)

                @pl.when((row == root - 1) & (p + 1 < panels))
                def _():
                    solve(p + 1, c, res_ref[tail:, columns(c)])

                    @pl.when(p + 1 < last)
                    def _():
                        for h in range(HALVES):
                            up(p + 1, c, h).start()

            @pl.when((row == helper) & (p < last))
            def _():
                far_sum[c] += product((fph[...], fpl[...]), ys, NN)

                @pl.when(p == last - 1)
                def _():
                    far_rows(c).wait_recv()
                    solve(last, c, far_own[c] - far_sum[c])
                    for h in range(HALVES):
                        up(last, c, h).start()

            @pl.when(row == root)
            def _():
                res_ref[tail:, columns(c)] = y[p, c]

            begin = jnp.where((row == last_root) & (p == last), panels, p)
            end = jnp.where((row == last_root) & (p == last - 1), panels, p + 1)

            @pl.loop(begin, end)
            def _(q):
                yq = split(y[q, c])
                for b in range(blocks - 1):
                    at = slice(b * width, (b + 1) * width)
                    res_ref[at, columns(c)] -= product((pth[q, at], ptl[q, at]), yq, NN)
                for b in range(blocks):
                    at = slice(b * width, (b + 1) * width)
                    grad[q, b] -= product(yq, (wh[c, at], wl[c, at]), NT)

            @pl.when((c == count // 2) & (p > 0))
            def _():
                chip_start(p - 1)

        @pl.when(row == root)
        def _():
            inner = lax.broadcasted_iota(jnp.int32, (width, width), 0)
            within = lax.broadcasted_iota(jnp.int32, (width, width), 1)
            grad[p, blocks - 1] = jnp.where(inner >= within, grad[p, blocks - 1], 0.0)

        pair_start(p)

        @pl.when((p > 0) & (p < last))
        def _():
            finish(p - 1)

    chip_start(last)
    finish(last - 1)
    finish(last)

    @pl.loop(0, panels)
    def _(p):
        root = n_row - 1 - p

        def act(g):
            for m in range(chips):
                pair_copy(p, m, g).wait_send()
            for j in range(1, chips):
                chip_copy(p, j, g).wait_send()

        groups(p, act)

        @pl.loop(0, count)
        def _(c):
            for h in range(HALVES):
                @pl.when((row >= root) & (row < n_row - 1) & ((p < last) | (row > last_root)))
                def _():
                    up(p, c, h).wait_send()

                @pl.when((row <= root) & (row > 0))
                def _():
                    down(p, c, h).wait_send()

    @pl.when(row == last_root)
    def _():
        @pl.loop(0, last)
        def _(p):
            far_panel(p).wait_send()

        @pl.loop(0, count)
        def _(c):
            far_rows(c).wait_send()


def store_kernel(res_ref, grad_ref, res_hbm, grad_hbm, sems):
    copies = (
        pltpu.make_async_copy(res_ref, res_hbm, sems.at[0]),
        pltpu.make_async_copy(grad_ref, grad_hbm, sems.at[1]),
    )
    for copy in copies:
        copy.start()
    for copy in copies:
        copy.wait()


def solution(mesh):
    n_row, n_col = mesh.shape["row"], mesh.shape["col"]

    def body(cotangent, whitened, panel_rows, diag_inverse):
        rows, rhs = cotangent.shape
        panels, width = diag_inverse.shape[:2]
        assert 3 <= panels <= n_row and n_col % 2 == 0
        count, blocks, part, chips = rhs // CHUNK, rows // width, width // n_col, n_col // 2
        vmem = pl.BlockSpec(memory_space=pltpu.VMEM)
        hbm = pl.BlockSpec(memory_space=pltpu.HBM)
        dma = pltpu.SemaphoreType.DMA
        kept = pl.pallas_call(
            functools.partial(kernel, n_row, n_col),
            out_shape=(pltpu.VMEM((rows, rhs), F32), pltpu.VMEM((panels, part, rows), F32)),
            in_specs=[hbm] * 4,
            out_specs=(vmem, vmem),
            scratch_shapes=[
                pltpu.VMEM((rows, rhs), F32),
                pltpu.VMEM((panels, width, rows), F32),
                pltpu.VMEM((panels, width, width), F32),
                pltpu.VMEM((panels, count, width, CHUNK), F32),
                pltpu.VMEM((panels, rows, width), BF16),
                pltpu.VMEM((panels, rows, width), BF16),
                pltpu.VMEM((panels, width, width), BF16),
                pltpu.VMEM((panels, width, width), BF16),
                pltpu.VMEM((count, rows, CHUNK), BF16),
                pltpu.VMEM((count, rows, CHUNK), BF16),
                pltpu.VMEM((panels, blocks, width, width), F32),
                pltpu.VMEM((panels, chips, blocks, part, width), F32),
                pltpu.VMEM((panels, chips, blocks, part, width), F32),
                pltpu.VMEM((panels - 1, width, width), F32),
                pltpu.VMEM((count, width, CHUNK), F32),
                pltpu.VMEM((count, width, CHUNK), F32),
                pltpu.VMEM((width, width), BF16),
                pltpu.VMEM((width, width), BF16),
                dma((5,)),
                dma((panels, count, HALVES)),
                dma((panels, count, HALVES)),
                dma((panels, count, HALVES)),
                dma((panels, chips, 2)),
                dma((panels, chips, 2)),
                dma((panels, chips, 2)),
                dma((panels, chips, 2)),
                dma((panels - 1,)),
                dma((panels - 1,)),
                dma((count,)),
                dma((count,)),
            ],
            compiler_params=pltpu.CompilerParams(
                collective_id=0, has_side_effects=True, vmem_limit_bytes=117 * 512 * 1024
            ),
        )(cotangent, whitened, panel_rows, diag_inverse)
        return pl.pallas_call(
            store_kernel,
            out_shape=tuple(jax.ShapeDtypeStruct(k.shape, F32) for k in kept),
            in_specs=[pl.BlockSpec(memory_space=pl.ANY)] * 2,
            out_specs=(hbm, hbm),
            scratch_shapes=[dma((2,))],
            compiler_params=pltpu.CompilerParams(vmem_limit_bytes=1024 * 1024),
        )(*kept)

    return jax.shard_map(
        body,
        mesh=mesh,
        in_specs=(P("row", "col"), P("row", "col"), P(None, None, "row"), P()),
        out_specs=(P("row", "col"), P(None, "col", "row")),
        check_vma=False,
    )
```

profile of v0, /device:TPU:0, one launch (start us, length us, event | category | flops | bytes accessed | tf_op | source)
XLA Modules:
  0.0 106.1 jit_solution(8189176966563102371)
XLA Ops:
  0.6 103.2 %shard_map.59 = (f32[1024,1024]{1,0:T(8,128)S(1)}, f32[4,32,1024]{2,1,0:T(8,128)S(1)}) custom-call(f32[1024,1024]{1,0:T(8,128)} %cot_hbm.1, f32[1024,1024]{1,0:T(8,128)} %wht_hbm.1, f32[4,256,1024]{2,1,0:T(8,128)} %pan_hbm.1, f32[4,256,256]{2,1,0:T(8,128)} %diag_hbm.1), custom_call_target="tpu_custom_call" | custom-call | tf_op jit(solution)/shard_map/pallas_call | solution.py:353
  103.9 2.2 %shard_map.60 = (f32[1024,1024]{1,0:T(8,128)}, f32[4,32,1024]{2,1,0:T(8,128)}) custom-call(f32[1024,1024]{1,0:T(8,128)S(1)} %get-tuple-element.4.res_ref, f32[4,32,1024]{2,1,0:T(8,128)S(1)} %get-tuple-element.5.grad_ref), custom_call_target="tpu_custom_call" | custom-call | tf_op jit(solution)/shard_map/pallas_call | solution.py:394
where the time goes:
time: 106 us
  Pallas kernels  105 us (99%)
    pallas_call x1, Pallas kernels, body(): pl.pallas_call(functools.partial(kernel, n_row, n_col), out_shape=(pltpu....  103 us
    pallas_call x1, Pallas kernels, body(): pl.pallas_call(store_kernel, out_shape=tuple((jax.ShapeDtypeStruct(k.shap...  2.19 us

commit v1 on v0

v1 whole, which is shorter than its diff:
```python
import functools

import jax
import jax.numpy as jnp
from jax import lax
from jax.experimental import pallas as pl
from jax.experimental.pallas import tpu as pltpu
from jax.sharding import PartitionSpec as P

MESH = pl.DeviceIdType.MESH
CHUNK = 128
PIECES = 2
LAG = 3
F32 = jnp.float32
BF16 = jnp.bfloat16


def split(x):
    hi = x.astype(BF16)
    return hi, (x - hi.astype(F32)).astype(BF16)


def product(a, b, dims):
    dot = functools.partial(lax.dot_general, dimension_numbers=(dims, ((), ())), preferred_element_type=F32)
    return dot(a[0], b[0]) + (dot(a[0], b[1]) + dot(a[1], b[0]))


NN = ((1,), (0,))
NT = ((1,), (1,))


def kernel(
    n_row, n_col, cot_hbm, wht_hbm, pan_hbm, diag_hbm, res_ref, out_ref,
    wht_ref, pan_ref, diag_ref, y, pth, ptl, dth, dtl, wh, wl, grad, rs_a, rs_b,
    far_pan, far_own, fph, fpl,
    local_sem, recv_sem, down_sem, up_sem, a_send, a_recv, b_send, b_recv, fp_send, fp_recv, fo_send, fo_recv,
):
    rows, rhs = res_ref.shape
    panels, width = diag_ref.shape[0], diag_ref.shape[1]
    count = rhs // CHUNK
    blocks = rows // width
    tail = rows - width
    part = width // n_col
    chips = n_col // 2
    piece = width // PIECES
    row, col = lax.axis_index("row"), lax.axis_index("col")
    core, chip = lax.rem(col, 2), col // 2
    last = panels - 1
    last_root = n_row - panels
    helper = last_root + 1

    def columns(c):
        return pl.ds(pl.multiple_of(c * CHUNK, CHUNK), CHUNK)

    def y_copy(p, c, h, sems, step):
        block = y.at[p, c, h * piece : (h + 1) * piece]
        return pltpu.make_async_remote_copy(
            src_ref=block, dst_ref=block, send_sem=sems.at[p], recv_sem=recv_sem.at[p, c, h],
            device_id={"row": lax.rem(row + step, n_row)}, device_id_type=MESH,
        )

    def down(p, c, h):
        return y_copy(p, c, h, down_sem, n_row - 1)

    def up(p, c, h):
        return y_copy(p, c, h, up_sem, 1)

    def far_panel(p):
        return pltpu.make_async_remote_copy(
            src_ref=pan_hbm.at[p, :, tail:], dst_ref=far_pan.at[p], send_sem=fp_send, recv_sem=fp_recv,
            device_id={"row": lax.rem(row + 1, n_row)}, device_id_type=MESH,
        )

    def far_rows(c):
        return pltpu.make_async_remote_copy(
            src_ref=cot_hbm.at[tail:, columns(c)], dst_ref=far_own.at[c], send_sem=fo_send, recv_sem=fo_recv.at[c],
            device_id={"row": lax.rem(row + 1, n_row)}, device_id_type=MESH,
        )

    def group(g):
        return slice(0, blocks - 1) if g == 0 else slice(blocks - 1, blocks)

    def pair_copy(p, m, g):
        place = (2 * m + 1 - core) * part
        return pltpu.make_async_remote_copy(
            src_ref=grad.at[p, group(g), pl.ds(pl.multiple_of(place, part), part)], dst_ref=rs_a.at[p, m, group(g)],
            send_sem=a_send.at[p, g], recv_sem=a_recv.at[p, g],
            device_id={"col": 2 * chip + 1 - core}, device_id_type=MESH,
        )

    def chip_copy(p, j, g):
        peer = lax.rem(chip + j, chips)
        return pltpu.make_async_remote_copy(
            src_ref=rs_a.at[p, peer, group(g)], dst_ref=rs_b.at[p, j, group(g)],
            send_sem=b_send.at[p, g], recv_sem=b_recv.at[p, g],
            device_id={"col": 2 * peer + core}, device_id_type=MESH,
        )

    def pair_all(p, g):
        return pltpu.make_async_remote_copy(
            src_ref=rs_a.at[p, :, group(g)], dst_ref=rs_a.at[p, :, group(g)],
            send_sem=a_send.at[p, g], recv_sem=a_recv.at[p, g],
            device_id={"col": 2 * chip + 1 - core}, device_id_type=MESH,
        )

    def chip_all(p, g):
        return pltpu.make_async_remote_copy(
            src_ref=rs_b.at[p, 1:, group(g)], dst_ref=rs_b.at[p, 1:, group(g)],
            send_sem=b_send.at[p, g], recv_sem=b_recv.at[p, g],
            device_id={"col": 2 * lax.rem(chip + 1, chips) + core}, device_id_type=MESH,
        )

    def y_all(p, sems, step):
        return pltpu.make_async_remote_copy(
            src_ref=y.at[p], dst_ref=y.at[p], send_sem=sems.at[p], recv_sem=recv_sem.at[p, 0, 0],
            device_id={"row": lax.rem(row + step, n_row)}, device_id_type=MESH,
        )

    def far_all():
        return pltpu.make_async_remote_copy(
            src_ref=far_pan, dst_ref=far_pan, send_sem=fp_send, recv_sem=fp_recv,
            device_id={"row": lax.rem(row + 1, n_row)}, device_id_type=MESH,
        )

    def own_all():
        return pltpu.make_async_remote_copy(
            src_ref=far_own, dst_ref=far_own, send_sem=fo_send, recv_sem=fo_recv.at[0],
            device_id={"row": lax.rem(row + 1, n_row)}, device_id_type=MESH,
        )

    def groups(p, act):
        act(0)

        @pl.when(row <= n_row - 1 - p)
        def _():
            act(1)

    def pair_start(p):
        @pl.when(row == n_row - 1 - p)
        def _():
            inner = lax.broadcasted_iota(jnp.int32, (width, width), 0)
            within = lax.broadcasted_iota(jnp.int32, (width, width), 1)
            grad[p, blocks - 1] = jnp.where(inner >= within, grad[p, blocks - 1], 0.0)

        def act(g):
            for m in range(chips):
                pair_copy(p, m, g).start()

        groups(p, act)

    def chip_start(p):
        def act(g):
            pair_all(p, g).wait_recv()
            for m in range(chips):
                place = pl.multiple_of((2 * m + core) * part, part)
                rs_a[p, m, group(g)] += grad[p, group(g), pl.ds(place, part)]
            for j in range(1, chips):
                chip_copy(p, j, g).start()

        groups(p, act)

    def finish(p):
        def act(g):
            chip_all(p, g).wait_recv()
            for b in range(blocks)[group(g)]:
                total = rs_a[p, chip, b]
                for j in range(1, chips):
                    total = total + rs_b[p, j, b]
                out_ref[p, :, b * width : (b + 1) * width] = total

        out_ref[p, :, tail:] = jnp.zeros((part, width), F32)
        groups(p, act)

    def solve(p, c, own):
        y[p, c] = product((dth[p], dtl[p]), split(own), NN)

    def inverse(p):
        hi, lo = split(diag_ref[p].T)
        dth[p] = hi
        dtl[p] = lo

    def receive(p, c):
        root = n_row - 1 - p
        source = row == root
        if p == last:
            source = source | (row == helper)
        for h in range(PIECES):
            @pl.when(jnp.logical_not(source))
            def _():
                y_copy(p, c, h, down_sem, n_row - 1).wait_recv()

            @pl.when(jnp.logical_not(source) & (row > root) & (row < n_row - 1))
            def _():
                up(p, c, h).start()

            @pl.when((row > 0) & (row < root))
            def _():
                down(p, c, h).start()

    def send(p, c, way):
        for h in range(PIECES):
            way(p, c, h).start()

    def tail_update(p, c):
        res_ref[tail:, columns(c)] -= product((pth[p, tail:], ptl[p, tail:]), split(y[p, c]), NN)

    def keep(p, c):
        @pl.when(row == n_row - 1 - p)
        def _():
            res_ref[tail:, columns(c)] = y[p, c]

    def grad_work(q, c):
        yq = split(y[q, c])
        for b in range(blocks):
            at = slice(b * width, (b + 1) * width)
            grad[q, b] -= product(yq, (wh[c, at], wl[c, at]), NT)

    def res_work(q, c):
        yq = split(y[q, c])
        for b in range(blocks - 1):
            at = slice(b * width, (b + 1) * width)
            res_ref[at, columns(c)] -= product((pth[q, at], ptl[q, at]), yq, NN)

    def far(c):
        far_rows(c).wait_recv()
        own = far_own[c]
        for p in range(last):
            own = own - product((fph[p], fpl[p]), split(y[p, c]), NN)
        solve(last, c, own)
        send(last, c, up)

    barrier = pltpu.get_barrier_semaphore()
    for step in (1, n_row - 1):
        pl.semaphore_signal(barrier, inc=1, device_id={"row": lax.rem(row + step, n_row)}, device_id_type=MESH)
    for step in range(1, n_col):
        pl.semaphore_signal(barrier, inc=1, device_id={"col": lax.rem(col + step, n_col)}, device_id_type=MESH)

    diag_copy = pltpu.make_async_copy(diag_hbm, diag_ref, local_sem.at[0])
    tail_copy = pltpu.make_async_copy(cot_hbm.at[tail:], res_ref.at[tail:], local_sem.at[1])
    pan_copy = pltpu.make_async_copy(pan_hbm, pan_ref, local_sem.at[2])
    head_copy = pltpu.make_async_copy(cot_hbm.at[:tail], res_ref.at[:tail], local_sem.at[3])
    wht_copy = pltpu.make_async_copy(wht_hbm, wht_ref, local_sem.at[4])
    for copy in (diag_copy, tail_copy, pan_copy, wht_copy, head_copy):
        copy.start()
    diag_copy.wait()
    inverse(0)
    tail_copy.wait()
    pl.semaphore_wait(barrier, 2 + n_col - 1)

    @pl.when(row == n_row - 1)
    def _():
        @pl.loop(0, count)
        def _(c):
            solve(0, c, res_ref[tail:, columns(c)])
            send(0, c, down)

    @pl.when(row == last_root)
    def _():
        @pl.loop(0, last)
        def _(p):
            far_panel(p).start()

        @pl.loop(0, count)
        def _(c):
            far_rows(c).start()

    @pl.loop(1, panels)
    def _(p):
        inverse(p)

    pan_copy.wait()

    @pl.loop(0, panels)
    def _(p):
        for b in range(blocks):
            hi, lo = split(pan_ref[p, :, b * width : (b + 1) * width].T)
            pth[p, b * width : (b + 1) * width] = hi
            ptl[p, b * width : (b + 1) * width] = lo
        grad[p] = jnp.zeros(grad.shape[1:], F32)

    wht_copy.wait()
    head_copy.wait()

    @pl.loop(0, count)
    def _(c):
        for p in range(last - 1):
            root = n_row - 1 - p
            receive(p, c)

            @pl.when(row < root)
            def _():
                tail_update(p, c)

                @pl.when(row == root - 1)
                def _():
                    solve(p + 1, c, res_ref[tail:, columns(c)])
                    send(p + 1, c, up)
                    if p + 1 < last - 1:
                        send(p + 1, c, down)

            keep(p, c)

        hi, lo = split(wht_ref[:, columns(c)])
        wh[c] = hi
        wl[c] = lo

        end = jnp.where(row == helper, last, last - 1)

        @pl.loop(0, end)
        def _(q):
            grad_work(q, c)
            res_work(q, c)

        @pl.when((row == helper) & (c == LAG))
        def _():
            far_all().wait_recv()

            @pl.loop(0, last)
            def _(p):
                hi, lo = split(far_pan[p].T)
                fph[p] = hi
                fpl[p] = lo

        @pl.when((row == helper) & (c >= LAG))
        def _():
            far(c - LAG)

    @pl.when(row == helper)
    def _():
        @pl.loop(0, count)
        def _(c):
            send(last - 1, c, down)

        @pl.loop(count - LAG, count)
        def _(c):
            far(c)

    for p in range(last - 1):
        pair_start(p)

    @pl.when(row == helper)
    def _():
        pair_start(last - 1)

    lag = jnp.where(row > helper, LAG, 0)

    @pl.loop(0, count + lag)
    def _(t):
        @pl.when((row != helper) & (t < count))
        def _():
            receive(last - 1, t)

            @pl.when(row < helper)
            def _():
                tail_update(last - 1, t)

                @pl.when(row == last_root)
                def _():
                    solve(last, t, res_ref[tail:, columns(t)])

                    @pl.when(row > 0)
                    def _():
                        send(last, t, down)

        @pl.when(t < count)
        def _():
            keep(last - 1, t)

        c = t - lag

        @pl.when(c >= 0)
        def _():
            receive(last, c)

            @pl.when(row < last_root)
            def _():
                tail_update(last, c)

            keep(last, c)

        @pl.when((row != helper) & (t < count))
        def _():
            grad_work(last - 1, t)

            @pl.when(t == count - 1)
            def _():
                pair_start(last - 1)

        @pl.when(c >= 0)
        def _():
            grad_work(last, c)

            @pl.when(c == count - 1)
            def _():
                pair_start(last)

        @pl.when((row != helper) & (t < count))
        def _():
            res_work(last - 1, t)

        @pl.when(c >= 0)
        def _():
            res_work(last, c)

        for p in range(last - 1):
            @pl.when(t == 1 + p)
            def _():
                chip_start(p)

            @pl.when(t == count - 3 + p)
            def _():
                finish(p)

        @pl.when((t == count + 1) | ((row == helper) & (t == count // 2)))
        def _():
            chip_start(last - 1)

    @pl.when(row < helper)
    def _():
        chip_start(last - 1)

    chip_start(last)
    finish(last - 1)
    finish(last)

    @pl.loop(0, panels)
    def _(p):
        root = n_row - 1 - p

        def act(g):
            pair_all(p, g).wait_send()
            chip_all(p, g).wait_send()

        groups(p, act)

        @pl.when((row >= root) & (row < n_row - 1) & ((p < last) | (row > last_root)))
        def _():
            y_all(p, up_sem, 1).wait_send()

        @pl.when((row <= root) & (row > 0))
        def _():
            y_all(p, down_sem, n_row - 1).wait_send()

    @pl.when(row == last_root)
    def _():
        far_all().wait_send()
        own_all().wait_send()


def store_kernel(res_ref, grad_ref, res_hbm, grad_hbm, sems):
    copies = (
        pltpu.make_async_copy(res_ref, res_hbm, sems.at[0]),
        pltpu.make_async_copy(grad_ref, grad_hbm, sems.at[1]),
    )
    for copy in copies:
        copy.start()
    for copy in copies:
        copy.wait()


def solution(mesh):
    n_row, n_col = mesh.shape["row"], mesh.shape["col"]

    def body(cotangent, whitened, panel_rows, diag_inverse):
        rows, rhs = cotangent.shape
        panels, width = diag_inverse.shape[:2]
        assert 3 <= panels <= n_row and n_col % 2 == 0 and rhs // CHUNK > LAG + 2
        count, blocks, part, chips = rhs // CHUNK, rows // width, width // n_col, n_col // 2
        anywhere = pl.BlockSpec(memory_space=pl.ANY)
        vmem = pl.BlockSpec(memory_space=pltpu.VMEM)
        hbm = pl.BlockSpec(memory_space=pltpu.HBM)
        dma = pltpu.SemaphoreType.DMA
        kept = pl.pallas_call(
            functools.partial(kernel, n_row, n_col),
            out_shape=(pltpu.VMEM((rows, rhs), F32), pltpu.VMEM((panels, part, rows), F32)),
            in_specs=[hbm] * 4,
            out_specs=(vmem, vmem),
            scratch_shapes=[
                pltpu.VMEM((rows, rhs), F32),
                pltpu.VMEM((panels, width, rows), F32),
                pltpu.VMEM((panels, width, width), F32),
                pltpu.VMEM((panels, count, width, CHUNK), F32),
                pltpu.VMEM((panels, rows, width), BF16),
                pltpu.VMEM((panels, rows, width), BF16),
                pltpu.VMEM((panels, width, width), BF16),
                pltpu.VMEM((panels, width, width), BF16),
                pltpu.VMEM((count, rows, CHUNK), BF16),
                pltpu.VMEM((count, rows, CHUNK), BF16),
                pltpu.VMEM((panels, blocks, width, width), F32),
                pltpu.VMEM((panels, chips, blocks, part, width), F32),
                pltpu.VMEM((panels, chips, blocks, part, width), F32),
                pltpu.VMEM((panels - 1, width, width), F32),
                pltpu.VMEM((count, width, CHUNK), F32),
                pltpu.VMEM((panels - 1, width, width), BF16),
                pltpu.VMEM((panels - 1, width, width), BF16),
                dma((5,)),
                dma((panels, count, PIECES)),
                dma((panels,)),
                dma((panels,)),
                dma((panels, 2)),
                dma((panels, 2)),
                dma((panels, 2)),
                dma((panels, 2)),
                dma,
                dma,
                dma,
                dma((count,)),
            ],
            compiler_params=pltpu.CompilerParams(
                collective_id=0, has_side_effects=True, vmem_limit_bytes=117 * 512 * 1024
            ),
        )(cotangent, whitened, panel_rows, diag_inverse)
        return pl.pallas_call(
            store_kernel,
            out_shape=tuple(jax.ShapeDtypeStruct(k.shape, F32) for k in kept),
            in_specs=[anywhere] * 2,
            out_specs=(hbm, hbm),
            scratch_shapes=[dma((2,))],
            compiler_params=pltpu.CompilerParams(vmem_limit_bytes=1024 * 1024),
        )(*kept)

    return jax.shard_map(
        body,
        mesh=mesh,
        in_specs=(P("row", "col"), P("row", "col"), P(None, None, "row"), P()),
        out_specs=(P("row", "col"), P(None, "col", "row")),
        check_vma=False,
    )
```

time: 106 us -> 106 us (level)
  no operation moved by 1% of the time
where the time goes in v1:
time: 106 us
  Pallas kernels  105 us (99%)
    pallas_call x1, Pallas kernels, body(): pl.pallas_call(functools.partial(kernel, n_row, n_col), out_shape=(pltpu....  103 us
    pallas_call x1, Pallas kernels, body(): pl.pallas_call(store_kernel, out_shape=tuple((jax.ShapeDtypeStruct(k.shap...  2.19 us

profile of v1, /device:TPU:0, one launch (start us, length us, event | category | flops | bytes accessed | tf_op | source)
XLA Modules:
  0.0 105.5 jit_solution(11769711504068537330)
XLA Ops:
  0.6 102.7 %shard_map.59 = (f32[1024,1024]{1,0:T(8,128)S(1)}, f32[4,32,1024]{2,1,0:T(8,128)S(1)}) custom-call(f32[1024,1024]{1,0:T(8,128)} %cot_hbm.1, f32[1024,1024]{1,0:T(8,128)} %wht_hbm.1, f32[4,256,1024]{2,1,0:T(8,128)} %pan_hbm.1, f32[4,256,256]{2,1,0:T(8,128)} %diag_hbm.1), custom_call_target="tpu_custom_call" | custom-call | tf_op jit(solution)/shard_map/pallas_call | solution.py:473
  103.3 2.2 %shard_map.60 = (f32[1024,1024]{1,0:T(8,128)}, f32[4,32,1024]{2,1,0:T(8,128)}) custom-call(f32[1024,1024]{1,0:T(8,128)S(1)} %get-tuple-element.4.res_ref, f32[4,32,1024]{2,1,0:T(8,128)S(1)} %get-tuple-element.5.grad_ref), custom_call_target="tpu_custom_call" | custom-call | tf_op jit(solution)/shard_map/pallas_call | solution.py:513

commit v2 on v1

--- a/solution.py
+++ b/solution.py
@@ -8,9 +8,11 @@
 from jax.sharding import PartitionSpec as P
 
 MESH = pl.DeviceIdType.MESH
-CHUNK = 128
-PIECES = 2
-LAG = 3
+CHUNK = 256
+PIECES = 4
+STORES = 4
+RAW = (0, 2)
+LATE = 1
 F32 = jnp.float32
 BF16 = jnp.bfloat16
 
@@ -32,8 +34,9 @@
 def kernel(
     n_row, n_col, cot_hbm, wht_hbm, pan_hbm, diag_hbm, res_ref, out_ref,
     wht_ref, pan_ref, diag_ref, y, pth, ptl, dth, dtl, wh, wl, grad, rs_a, rs_b,
-    far_pan, far_own, fph, fpl,
-    local_sem, recv_sem, down_sem, up_sem, a_send, a_recv, b_send, b_recv, fp_send, fp_recv, fo_send, fo_recv,
+    far_pan, far_own, fph, fpl, late_w, late_out, late_in,
+    local_sem, recv_sem, down_sem, up_sem, a_send, a_recv, b_send, b_recv,
+    fp_send, fp_recv, fo_send, fo_recv, ag_send, ag_recv, lw_send, lw_recv, lr_send, lr_recv,
 ):
     rows, rhs = res_ref.shape
     panels, width = diag_ref.shape[0], diag_ref.shape[1]
@@ -65,16 +68,45 @@
     def up(p, c, h):
         return y_copy(p, c, h, up_sem, 1)
 
-    def far_panel(p):
-        return pltpu.make_async_remote_copy(
-            src_ref=pan_hbm.at[p, :, tail:], dst_ref=far_pan.at[p], send_sem=fp_send, recv_sem=fp_recv,
+    own_part = pl.ds(pl.multiple_of(col * part, part), part)
+
+    def panel_part(n, step):
+        return pltpu.make_async_remote_copy(
+            src_ref=pan_hbm.at[:n, own_part, tail:], dst_ref=far_pan.at[:n, own_part],
+            send_sem=fp_send, recv_sem=fp_recv,
+            device_id={"row": lax.rem(row + step, n_row)}, device_id_type=MESH,
+        )
+
+    def panel_share(n, step):
+        return pltpu.make_async_remote_copy(
+            src_ref=far_pan.at[:n, own_part], dst_ref=far_pan.at[:n, own_part],
+            send_sem=ag_send, recv_sem=ag_recv,
+            device_id={"col": lax.rem(col + step, n_col)}, device_id_type=MESH,
+        )
+
+    def panel_shares(n):
+        others = far_pan.at[:n, : (n_col - 1) * part]
+        return pltpu.make_async_remote_copy(
+            src_ref=others, dst_ref=others, send_sem=ag_send, recv_sem=ag_recv,
+            device_id={"col": lax.rem(col + 1, n_col)}, device_id_type=MESH,
+        )
+
+    def far_rows(c, step):
+        return pltpu.make_async_remote_copy(
+            src_ref=cot_hbm.at[tail:, columns(c)], dst_ref=far_own.at[c], send_sem=fo_send, recv_sem=fo_recv.at[c],
+            device_id={"row": lax.rem(row + step, n_row)}, device_id_type=MESH,
+        )
+
+    def late_rows():
+        return pltpu.make_async_remote_copy(
+            src_ref=wht_hbm.at[:, columns(LATE)], dst_ref=late_w, send_sem=lw_send, recv_sem=lw_recv,
             device_id={"row": lax.rem(row + 1, n_row)}, device_id_type=MESH,
         )
 
-    def far_rows(c):
-        return pltpu.make_async_remote_copy(
-            src_ref=cot_hbm.at[tail:, columns(c)], dst_ref=far_own.at[c], send_sem=fo_send, recv_sem=fo_recv.at[c],
-            device_id={"row": lax.rem(row + 1, n_row)}, device_id_type=MESH,
+    def late_result():
+        return pltpu.make_async_remote_copy(
+            src_ref=late_out, dst_ref=late_in, send_sem=lr_send, recv_sem=lr_recv,
+            device_id={"row": lax.rem(row + n_row - 1, n_row)}, device_id_type=MESH,
         )
 
     def group(g):
@@ -110,16 +142,10 @@
             device_id={"col": 2 * lax.rem(chip + 1, chips) + core}, device_id_type=MESH,
         )
 
-    def y_all(p, sems, step):
-        return pltpu.make_async_remote_copy(
-            src_ref=y.at[p], dst_ref=y.at[p], send_sem=sems.at[p], recv_sem=recv_sem.at[p, 0, 0],
+    def y_all(p, first, sems, step):
+        return pltpu.make_async_remote_copy(
+            src_ref=y.at[p, first:], dst_ref=y.at[p, first:], send_sem=sems.at[p], recv_sem=recv_sem.at[p, 0, 0],
             device_id={"row": lax.rem(row + step, n_row)}, device_id_type=MESH,
-        )
-
-    def far_all():
-        return pltpu.make_async_remote_copy(
-            src_ref=far_pan, dst_ref=far_pan, send_sem=fp_send, recv_sem=fp_recv,
-            device_id={"row": lax.rem(row + 1, n_row)}, device_id_type=MESH,
         )
 
     def own_all():
@@ -131,16 +157,19 @@
     def groups(p, act):
         act(0)
 
-        @pl.when(row <= n_row - 1 - p)
+        @pl.when((row <= n_row - 1 - p) | (p >= panels))
         def _():
             act(1)
+
+    def lower(p):
+        inner = lax.broadcasted_iota(jnp.int32, (width, width), 0)
+        within = lax.broadcasted_iota(jnp.int32, (width, width), 1)
+        grad[p, blocks - 1] = jnp.where(inner >= within, grad[p, blocks - 1], 0.0)
 
     def pair_start(p):
         @pl.when(row == n_row - 1 - p)
         def _():
-            inner = lax.broadcasted_iota(jnp.int32, (width, width), 0)
-            within = lax.broadcasted_iota(jnp.int32, (width, width), 1)
-            grad[p, blocks - 1] = jnp.where(inner >= within, grad[p, blocks - 1], 0.0)
+            lower(p)
 
         def act(g):
             for m in range(chips):
@@ -159,17 +188,35 @@
 
         groups(p, act)
 
+    def total(p, b):
+        value = rs_a[p, chip, b]
+        for j in range(1, chips):
+            value = value + rs_b[p, j, b]
+        return value
+
     def finish(p):
         def act(g):
             chip_all(p, g).wait_recv()
             for b in range(blocks)[group(g)]:
-                total = rs_a[p, chip, b]
-                for j in range(1, chips):
-                    total = total + rs_b[p, j, b]
-                out_ref[p, :, b * width : (b + 1) * width] = total
+                out_ref[p, :, b * width : (b + 1) * width] = total(p, b)
 
         out_ref[p, :, tail:] = jnp.zeros((part, width), F32)
         groups(p, act)
+
+    def late_work():
+        late_rows().wait_recv()
+        yq = split(y[last, LATE])
+        for b in range(blocks):
+            grad[panels, b] = -product(yq, split(late_w[b * width : (b + 1) * width]), NT)
+        lower(panels)
+        pair_start(panels)
+
+    def late_finish():
+        for g in range(2):
+            chip_all(panels, g).wait_recv()
+        for b in range(blocks):
+            late_out[:, b * width : (b + 1) * width] = total(panels, b)
+        late_result().start()
 
     def solve(p, c, own):
         y[p, c] = product((dth[p], dtl[p]), split(own), NN)
@@ -184,6 +231,10 @@
         source = row == root
         if p == last:
             source = source | (row == helper)
+        if p == last - 1:
+            source = source | ((row == last_root) & ((c == RAW[0]) | (c == RAW[1])))
+        if p == 1:
+            source = source | (row == n_row - 1)
         for h in range(PIECES):
             @pl.when(jnp.logical_not(source))
             def _():
@@ -221,13 +272,52 @@
             at = slice(b * width, (b + 1) * width)
             res_ref[at, columns(c)] -= product((pth[q, at], ptl[q, at]), yq, NN)
 
-    def far(c):
-        far_rows(c).wait_recv()
+    def take_panels(n):
+        panel_shares(n).wait_recv()
+        for p in range(n):
+            hi, lo = split(far_pan[p].T)
+            fph[p] = hi
+            fpl[p] = lo
+
+    def far(q, c):
+        far_rows(c, 1).wait_recv()
         own = far_own[c]
-        for p in range(last):
+        for p in range(q):
             own = own - product((fph[p], fpl[p]), split(y[p, c]), NN)
-        solve(last, c, own)
-        send(last, c, up)
+        solve(q, c, own)
+
+    def advance(p, c):
+        root = n_row - 1 - p
+        receive(p, c)
+
+        @pl.when(row < root)
+        def _():
+            tail_update(p, c)
+
+            @pl.when(row == root - 1)
+            def _():
+                solve(p + 1, c, res_ref[tail:, columns(c)])
+                if p + 1 < last - 1:
+                    send(p + 1, c, down)
+
+                if p > 0:
+                    send(p + 1, c, up)
+
+        keep(p, c)
+
+    def close(c):
+        receive(last - 1, c)
+        tail_update(last - 1, c)
+        solve(last, c, res_ref[tail:, columns(c)])
+
+        @pl.when(row > 0)
+        def _():
+            send(last, c, down)
+
+        keep(last, c)
+        for q in (last, last - 1):
+            grad_work(q, c)
+            res_work(q, c)
 
     barrier = pltpu.get_barrier_semaphore()
     for step in (1, n_row - 1):
@@ -254,15 +344,30 @@
             solve(0, c, res_ref[tail:, columns(c)])
             send(0, c, down)
 
-    @pl.when(row == last_root)
-    def _():
-        @pl.loop(0, last)
-        def _(p):
-            far_panel(p).start()
+    @pl.when(row == helper)
+    def _():
+        panel_part(last - 1, n_row - 1).start()
+        for c in RAW:
+            far_rows(c, n_row - 1).start()
+
+    @pl.when(row == n_row - 2)
+    def _():
+        panel_part(1, 1).start()
 
         @pl.loop(0, count)
         def _(c):
-            far_rows(c).start()
+            far_rows(c, 1).start()
+
+    @pl.when(row == last_root)
+    def _():
+        panel_part(last, 1).start()
+        for c in range(LATE + 1):
+            far_rows(c, 1).start()
+        late_rows().start()
+
+        @pl.loop(LATE + 1, count)
+        def _(c):
+            far_rows(c, 1).start()
 
     @pl.loop(1, panels)
     def _(p):
@@ -278,150 +383,218 @@
             ptl[p, b * width : (b + 1) * width] = lo
         grad[p] = jnp.zeros(grad.shape[1:], F32)
 
+    def share_panels(n, step):
+        panel_part(n, step).wait_recv()
+        for k in range(1, n_col):
+            panel_share(n, k).start()
+
+    @pl.when(row == helper)
+    def _():
+        share_panels(last, 1)
+
+    @pl.when(row == last_root)
+    def _():
+        share_panels(last - 1, n_row - 1)
+
+    @pl.when(row == n_row - 1)
+    def _():
+        share_panels(1, 1)
+
     wht_copy.wait()
     head_copy.wait()
+    advance(0, 0)
+
+    @pl.when(row == n_row - 1)
+    def _():
+        take_panels(1)
+
+    spared = row == last_root
+
+    @pl.when(row == helper)
+    def _():
+        take_panels(last)
+
+    passing = (row > helper) & (row < n_row - 1)
 
     @pl.loop(0, count)
     def _(c):
-        for p in range(last - 1):
-            root = n_row - 1 - p
-            receive(p, c)
-
-            @pl.when(row < root)
-            def _():
-                tail_update(p, c)
-
-                @pl.when(row == root - 1)
-                def _():
-                    solve(p + 1, c, res_ref[tail:, columns(c)])
-                    send(p + 1, c, up)
-                    if p + 1 < last - 1:
-                        send(p + 1, c, down)
-
-            keep(p, c)
+        @pl.when(passing & (c == count - 1))
+        def _():
+            receive(last - 1, 0)
 
         hi, lo = split(wht_ref[:, columns(c)])
         wh[c] = hi
         wl[c] = lo
-
-        end = jnp.where(row == helper, last, last - 1)
-
-        @pl.loop(0, end)
-        def _(q):
+        grad_work(0, c)
+
+        @pl.when(c == count - 1)
+        def _():
+            pair_start(0)
+
+        res_work(0, c)
+
+        @pl.when(c == count - 1)
+        def _():
+            chip_start(0)
+
+        @pl.when(row == n_row - 1)
+        def _():
+            far(1, c)
+
+        for p in range(1, last - 1):
+            advance(p, c)
+
+        @pl.when(row == helper)
+        def _():
+            @pl.when(c == count - 1)
+            def _():
+                @pl.loop(RAW[1] + 1, count)
+                def _(k):
+                    send(last - 1, k, down)
+
+                send(last - 1, LATE, down)
+
+            far(last, c)
+            send(last, c, up)
+
+            @pl.when(c == count - 1)
+            def _():
+                chip_start(panels)
+
+        for q in range(1, last - 1):
             grad_work(q, c)
+
+            @pl.when(c == count - 1)
+            def _():
+                pair_start(q)
+
             res_work(q, c)
 
-        @pl.when((row == helper) & (c == LAG))
-        def _():
-            far_all().wait_recv()
-
-            @pl.loop(0, last)
-            def _(p):
-                hi, lo = split(far_pan[p].T)
-                fph[p] = hi
-                fpl[p] = lo
-
-        @pl.when((row == helper) & (c >= LAG))
-        def _():
-            far(c - LAG)
+        @pl.when(spared & (c >= 1) & (c <= 2))
+        def _():
+            @pl.when(c == 1)
+            def _():
+                take_panels(last - 1)
+
+            r = (c - 1) * (RAW[1] - RAW[0]) + RAW[0]
+            far(last - 1, r)
+            close(r)
+
+        @pl.when(c + 1 < count)
+        def _():
+            advance(0, c + 1)
+
+        @pl.when(row == helper)
+        def _():
+            grad_work(last - 1, c)
+            res_work(last - 1, c)
+
+            @pl.when(c == LATE + 1)
+            def _():
+                late_work()
+
+    for p in range(1, last - 1):
+        chip_start(p)
 
     @pl.when(row == helper)
     def _():
-        @pl.loop(0, count)
-        def _(c):
-            send(last - 1, c, down)
-
-        @pl.loop(count - LAG, count)
-        def _(c):
-            far(c)
-
-    for p in range(last - 1):
-        pair_start(p)
-
-    @pl.when(row == helper)
-    def _():
         pair_start(last - 1)
 
-    lag = jnp.where(row > helper, LAG, 0)
-
-    @pl.loop(0, count + lag)
+    below = row < helper
+    start = jnp.where(spared, len(RAW), 0)
+    bulk = jnp.where(spared, count - 2, count - 1)
+
+    @pl.loop(start, count)
     def _(t):
-        @pl.when((row != helper) & (t < count))
-        def _():
-            receive(last - 1, t)
-
-            @pl.when(row < helper)
-            def _():
-                tail_update(last - 1, t)
-
-                @pl.when(row == last_root)
+        c = jnp.where(below & (t > 0), jnp.where(t == count - 1, LATE, t + 1), t)
+
+        @pl.when(t > bulk)
+        def _():
+            chip_start(last)
+
+        @pl.when((row != helper) & ((t > 0) | jnp.logical_not(passing)))
+        def _():
+            receive(last - 1, c)
+
+            @pl.when(below)
+            def _():
+                tail_update(last - 1, c)
+
+                @pl.when(spared)
                 def _():
-                    solve(last, t, res_ref[tail:, columns(t)])
+                    solve(last, c, res_ref[tail:, columns(c)])
 
                     @pl.when(row > 0)
                     def _():
-                        send(last, t, down)
-
-        @pl.when(t < count)
-        def _():
-            keep(last - 1, t)
-
-        c = t - lag
-
-        @pl.when(c >= 0)
-        def _():
-            receive(last, c)
-
-            @pl.when(row < last_root)
-            def _():
-                tail_update(last, c)
-
-            keep(last, c)
-
-        @pl.when((row != helper) & (t < count))
-        def _():
-            grad_work(last - 1, t)
+                        send(last, c, down)
+
+        keep(last - 1, c)
+
+        @pl.when(row > helper)
+        def _():
+            grad_work(last - 1, c)
 
             @pl.when(t == count - 1)
             def _():
                 pair_start(last - 1)
 
-        @pl.when(c >= 0)
+            res_work(last - 1, c)
+
+        receive(last, c)
+
+        @pl.when(row < last_root)
+        def _():
+            tail_update(last, c)
+
+        keep(last, c)
+
+        @pl.when((row >= helper) & (t == count - 1))
+        def _():
+            chip_start(last - 1)
+
+        @pl.when(t <= bulk)
         def _():
             grad_work(last, c)
 
-            @pl.when(c == count - 1)
+            @pl.when(t == bulk)
             def _():
                 pair_start(last)
 
-        @pl.when((row != helper) & (t < count))
-        def _():
-            res_work(last - 1, t)
-
-        @pl.when(c >= 0)
-        def _():
-            res_work(last, c)
-
-        for p in range(last - 1):
-            @pl.when(t == 1 + p)
-            def _():
-                chip_start(p)
-
-            @pl.when(t == count - 3 + p)
-            def _():
-                finish(p)
-
-        @pl.when((t == count + 1) | ((row == helper) & (t == count // 2)))
-        def _():
-            chip_start(last - 1)
-
-    @pl.when(row < helper)
+        @pl.when(below)
+        def _():
+            grad_work(last - 1, c)
+
+            @pl.when(t == count - 1)
+            def _():
+                pair_start(last - 1)
+
+            res_work(last - 1, c)
+
+        res_work(last, c)
+
+    @pl.when(below)
     def _():
         chip_start(last - 1)
 
-    chip_start(last)
+    @pl.when(jnp.logical_not(spared))
+    def _():
+        chip_start(last)
+
+    for p in range(last - 1):
+        finish(p)
+
+    @pl.when(row == helper)
+    def _():
+        late_finish()
+
+    finish(last)
     finish(last - 1)
-    finish(last)
+
+    @pl.when(spared)
+    def _():
+        late_result().wait_recv()
+        out_ref[last] += late_in[...]
+
 
     @pl.loop(0, panels)
     def _(p):
@@ -433,25 +606,49 @@
 
         groups(p, act)
 
-        @pl.when((row >= root) & (row < n_row - 1) & ((p < last) | (row > last_root)))
-        def _():
-            y_all(p, up_sem, 1).wait_send()
-
-        @pl.when((row <= root) & (row > 0))
-        def _():
-            y_all(p, down_sem, n_row - 1).wait_send()
-
-    @pl.when(row == last_root)
-    def _():
-        far_all().wait_send()
+        @pl.when((row >= root) & (row < n_row - 1) & ((p < last) | (row > last_root)) & (p != 1))
+        def _():
+            y_all(p, 0, up_sem, 1).wait_send()
+
+        @pl.when((row <= root) & (row > 0) & ((p != last - 1) | (row != helper)))
+        def _():
+            y_all(p, 0, down_sem, n_row - 1).wait_send()
+
+    @pl.when(row == helper)
+    def _():
+        y_all(last - 1, len(RAW), down_sem, n_row - 1).wait_send()
+        panel_part(last - 1, n_row - 1).wait_send()
+        for c in RAW:
+            far_rows(c, n_row - 1).wait_send()
+        panel_shares(last).wait_send()
+        late_result().wait_send()
+        for g in range(2):
+            pair_all(panels, g).wait_send()
+            chip_all(panels, g).wait_send()
+
+    @pl.when(row == n_row - 2)
+    def _():
+        panel_part(1, 1).wait_send()
         own_all().wait_send()
 
+    @pl.when(row == n_row - 1)
+    def _():
+        panel_shares(1).wait_send()
+
+    @pl.when(spared)
+    def _():
+        panel_part(last, 1).wait_send()
+        own_all().wait_send()
+        panel_shares(last - 1).wait_send()
+        late_rows().wait_send()
+
 
 def store_kernel(res_ref, grad_ref, res_hbm, grad_hbm, sems):
-    copies = (
-        pltpu.make_async_copy(res_ref, res_hbm, sems.at[0]),
-        pltpu.make_async_copy(grad_ref, grad_hbm, sems.at[1]),
-    )
+    step = res_ref.shape[0] // STORES
+    copies = [pltpu.make_async_copy(grad_ref, grad_hbm, sems.at[STORES])]
+    for k in range(STORES):
+        at = slice(k * step, (k + 1) * step)
+        copies.append(pltpu.make_async_copy(res_ref.at[at], res_hbm.at[at], sems.at[k]))
     for copy in copies:
         copy.start()
     for copy in copies:
@@ -464,7 +661,7 @@
     def body(cotangent, whitened, panel_rows, diag_inverse):
         rows, rhs = cotangent.shape
         panels, width = diag_inverse.shape[:2]
-        assert 3 <= panels <= n_row and n_col % 2 == 0 and rhs // CHUNK > LAG + 2
+        assert 3 <= panels <= n_row and n_col % 2 == 0 and rhs // CHUNK > RAW[1] + 1
         count, blocks, part, chips = rhs // CHUNK, rows // width, width // n_col, n_col // 2
         anywhere = pl.BlockSpec(memory_space=pl.ANY)
         vmem = pl.BlockSpec(memory_space=pltpu.VMEM)
@@ -486,25 +683,34 @@
                 pltpu.VMEM((panels, width, width), BF16),
                 pltpu.VMEM((count, rows, CHUNK), BF16),
                 pltpu.VMEM((count, rows, CHUNK), BF16),
-                pltpu.VMEM((panels, blocks, width, width), F32),
-                pltpu.VMEM((panels, chips, blocks, part, width), F32),
-                pltpu.VMEM((panels, chips, blocks, part, width), F32),
+                pltpu.VMEM((panels + 1, blocks, width, width), F32),
+                pltpu.VMEM((panels + 1, chips, blocks, part, width), F32),
+                pltpu.VMEM((panels + 1, chips, blocks, part, width), F32),
                 pltpu.VMEM((panels - 1, width, width), F32),
                 pltpu.VMEM((count, width, CHUNK), F32),
                 pltpu.VMEM((panels - 1, width, width), BF16),
                 pltpu.VMEM((panels - 1, width, width), BF16),
+                pltpu.VMEM((rows, CHUNK), F32),
+                pltpu.VMEM((part, rows), F32),
+                pltpu.VMEM((part, rows), F32),
                 dma((5,)),
                 dma((panels, count, PIECES)),
                 dma((panels,)),
                 dma((panels,)),
-                dma((panels, 2)),
-                dma((panels, 2)),
-                dma((panels, 2)),
-                dma((panels, 2)),
+                dma((panels + 1, 2)),
+                dma((panels + 1, 2)),
+                dma((panels + 1, 2)),
+                dma((panels + 1, 2)),
                 dma,
                 dma,
                 dma,
                 dma((count,)),
+                dma,
+                dma,
+                dma,
+                dma,
+                dma,
+                dma,
             ],
             compiler_params=pltpu.CompilerParams(
                 collective_id=0, has_side_effects=True, vmem_limit_bytes=117 * 512 * 1024
@@ -515,7 +721,7 @@
             out_shape=tuple(jax.ShapeDtypeStruct(k.shape, F32) for k in kept),
             in_specs=[anywhere] * 2,
             out_specs=(hbm, hbm),
-            scratch_shapes=[dma((2,))],
+            scratch_shapes=[dma((STORES + 1,))],
             compiler_params=pltpu.CompilerParams(vmem_limit_bytes=1024 * 1024),
         )(*kept)
 

time: 106 us -> 90.7 us (0.86)
  Pallas kernels: 105 us -> 89.8 us
    pallas_call x1, Pallas kernels: 103 us -> 87.6 us  [body(): pl.pallas_call(functools.partial(kernel, n_row, n_col), out_shape=(pltpu....]
where the time goes in v2:
time: 90.7 us; the launch traced here: 90.6 us
  Pallas kernels  89.8 us (99%)
    pallas_call x1, Pallas kernels, body(): pl.pallas_call(functools.partial(kernel, n_row, n_col), out_shape=(pltpu....  87.6 us
    pallas_call x1, Pallas kernels, body(): pl.pallas_call(store_kernel, out_shape=tuple((jax.ShapeDtypeStruct(k.shap...  2.22 us

profile of v2, /device:TPU:0, one launch (start us, length us, event | category | flops | bytes accessed | tf_op | source)
XLA Modules:
  0.0 90.6 jit_solution(2500003300509505162)
XLA Ops:
  0.6 87.6 %shard_map.59 = (f32[1024,1024]{1,0:T(8,128)S(1)}, f32[4,32,1024]{2,1,0:T(8,128)S(1)}) custom-call(f32[1024,1024]{1,0:T(8,128)} %cot_hbm.1, f32[1024,1024]{1,0:T(8,128)} %wht_hbm.1, f32[4,256,1024]{2,1,0:T(8,128)} %pan_hbm.1, f32[4,256,256]{2,1,0:T(8,128)} %diag_hbm.1), custom_call_target="tpu_custom_call" | custom-call | tf_op jit(solution)/shard_map/pallas_call | solution.py:670
  88.2 2.2 %shard_map.60 = (f32[1024,1024]{1,0:T(8,128)}, f32[4,32,1024]{2,1,0:T(8,128)}) custom-call(f32[1024,1024]{1,0:T(8,128)S(1)} %get-tuple-element.4.res_ref, f32[4,32,1024]{2,1,0:T(8,128)S(1)} %get-tuple-element.5.grad_ref), custom_call_target="tpu_custom_call" | custom-call | tf_op jit(solution)/shard_map/pallas_call | solution.py:719

commit v3 on v2

--- a/solution.py
+++ b/solution.py
@@ -58,7 +58,7 @@
     def y_copy(p, c, h, sems, step):
         block = y.at[p, c, h * piece : (h + 1) * piece]
         return pltpu.make_async_remote_copy(
-            src_ref=block, dst_ref=block, send_sem=sems.at[p], recv_sem=recv_sem.at[p, c, h],
+            src_ref=block, dst_ref=block, send_sem=sems, recv_sem=recv_sem.at[p, c, h],
             device_id={"row": lax.rem(row + step, n_row)}, device_id_type=MESH,
         )
 
@@ -116,7 +116,7 @@
         place = (2 * m + 1 - core) * part
         return pltpu.make_async_remote_copy(
             src_ref=grad.at[p, group(g), pl.ds(pl.multiple_of(place, part), part)], dst_ref=rs_a.at[p, m, group(g)],
-            send_sem=a_send.at[p, g], recv_sem=a_recv.at[p, g],
+            send_sem=a_send, recv_sem=a_recv.at[p, g],
             device_id={"col": 2 * chip + 1 - core}, device_id_type=MESH,
         )
 
@@ -124,27 +124,27 @@
         peer = lax.rem(chip + j, chips)
         return pltpu.make_async_remote_copy(
             src_ref=rs_a.at[p, peer, group(g)], dst_ref=rs_b.at[p, j, group(g)],
-            send_sem=b_send.at[p, g], recv_sem=b_recv.at[p, g],
+            send_sem=b_send, recv_sem=b_recv.at[p, g],
             device_id={"col": 2 * peer + core}, device_id_type=MESH,
         )
 
     def pair_all(p, g):
         return pltpu.make_async_remote_copy(
             src_ref=rs_a.at[p, :, group(g)], dst_ref=rs_a.at[p, :, group(g)],
-            send_sem=a_send.at[p, g], recv_sem=a_recv.at[p, g],
+            send_sem=a_send, recv_sem=a_recv.at[p, g],
             device_id={"col": 2 * chip + 1 - core}, device_id_type=MESH,
         )
 
     def chip_all(p, g):
         return pltpu.make_async_remote_copy(
             src_ref=rs_b.at[p, 1:, group(g)], dst_ref=rs_b.at[p, 1:, group(g)],
-            send_sem=b_send.at[p, g], recv_sem=b_recv.at[p, g],
+            send_sem=b_send, recv_sem=b_recv.at[p, g],
             device_id={"col": 2 * lax.rem(chip + 1, chips) + core}, device_id_type=MESH,
         )
 
     def y_all(p, first, sems, step):
         return pltpu.make_async_remote_copy(
-            src_ref=y.at[p, first:], dst_ref=y.at[p, first:], send_sem=sems.at[p], recv_sem=recv_sem.at[p, 0, 0],
+            src_ref=y.at[p, first:], dst_ref=y.at[p, first:], send_sem=sems, recv_sem=recv_sem.at[p, 0, 0],
             device_id={"row": lax.rem(row + step, n_row)}, device_id_type=MESH,
         )
 
@@ -508,13 +508,14 @@
     def _(t):
         c = jnp.where(below & (t > 0), jnp.where(t == count - 1, LATE, t + 1), t)
 
-        @pl.when(t > bulk)
-        def _():
-            chip_start(last)
-
         @pl.when((row != helper) & ((t > 0) | jnp.logical_not(passing)))
         def _():
             receive(last - 1, c)
+
+            @pl.when(t > bulk)
+            def _():
+                grad_work(last - 1, c)
+                pair_start(last - 1)
 
             @pl.when(below)
             def _():
@@ -540,6 +541,10 @@
 
             res_work(last - 1, c)
 
+            @pl.when((row == n_row - 1) & (t == count - 1))
+            def _():
+                chip_start(last - 1)
+
         receive(last, c)
 
         @pl.when(row < last_root)
@@ -548,7 +553,7 @@
 
         keep(last, c)
 
-        @pl.when((row >= helper) & (t == count - 1))
+        @pl.when(((row >= helper) & (row < n_row - 1) & (t == count - 1)) | (t > bulk))
         def _():
             chip_start(last - 1)
 
@@ -560,19 +565,25 @@
             def _():
                 pair_start(last)
 
+        @pl.when(below & (t <= bulk))
+        def _():
+            grad_work(last - 1, c)
+
+            @pl.when(t == count - 1)
+            def _():
+                pair_start(last - 1)
+
+            @pl.when(spared & (t == bulk))
+            def _():
+                chip_start(last)
+
         @pl.when(below)
         def _():
-            grad_work(last - 1, c)
-
-            @pl.when(t == count - 1)
-            def _():
-                pair_start(last - 1)
-
             res_work(last - 1, c)
 
         res_work(last, c)
 
-    @pl.when(below)
+    @pl.when(row < last_root)
     def _():
         chip_start(last - 1)
 
@@ -695,11 +706,11 @@
                 pltpu.VMEM((part, rows), F32),
                 dma((5,)),
                 dma((panels, count, PIECES)),
-                dma((panels,)),
-                dma((panels,)),
+                dma,
+                dma,
+                dma,
                 dma((panels + 1, 2)),
-                dma((panels + 1, 2)),
-                dma((panels + 1, 2)),
+                dma,
                 dma((panels + 1, 2)),
                 dma,
                 dma,

time: 90.7 us -> 89.9 us (level)
  no operation moved by 1% of the time
where the time goes in v3:
time: 89.9 us; the launch traced here: 89.8 us
  Pallas kernels  89 us (99%)
    pallas_call x1, Pallas kernels, body(): pl.pallas_call(functools.partial(kernel, n_row, n_col), out_shape=(pltpu....  86.8 us
    pallas_call x1, Pallas kernels, body(): pl.pallas_call(store_kernel, out_shape=tuple((jax.ShapeDtypeStruct(k.shap...  2.22 us

profile of v3, /device:TPU:0, one launch (start us, length us, event | category | flops | bytes accessed | tf_op | source)
XLA Modules:
  0.0 89.8 jit_solution(12008945282127737917)
XLA Ops:
  0.6 86.8 %shard_map.59 = (f32[1024,1024]{1,0:T(8,128)S(1)}, f32[4,32,1024]{2,1,0:T(8,128)S(1)}) custom-call(f32[1024,1024]{1,0:T(8,128)} %cot_hbm.1, f32[1024,1024]{1,0:T(8,128)} %wht_hbm.1, f32[4,256,1024]{2,1,0:T(8,128)} %pan_hbm.1, f32[4,256,256]{2,1,0:T(8,128)} %diag_hbm.1), custom_call_target="tpu_custom_call" | custom-call | tf_op jit(solution)/shard_map/pallas_call | solution.py:681
  87.4 2.2 %shard_map.60 = (f32[1024,1024]{1,0:T(8,128)}, f32[4,32,1024]{2,1,0:T(8,128)}) custom-call(f32[1024,1024]{1,0:T(8,128)S(1)} %get-tuple-element.4.res_ref, f32[4,32,1024]{2,1,0:T(8,128)S(1)} %get-tuple-element.5.grad_ref), custom_call_target="tpu_custom_call" | custom-call | tf_op jit(solution)/shard_map/pallas_call | solution.py:730

commit v4 on v3

--- a/solution.py
+++ b/solution.py
@@ -9,7 +9,7 @@
 
 MESH = pl.DeviceIdType.MESH
 CHUNK = 256
-PIECES = 4
+PIECES = (4, 4, 2, 4)
 STORES = 4
 RAW = (0, 2)
 LATE = 1
@@ -34,9 +34,9 @@
 def kernel(
     n_row, n_col, cot_hbm, wht_hbm, pan_hbm, diag_hbm, res_ref, out_ref,
     wht_ref, pan_ref, diag_ref, y, pth, ptl, dth, dtl, wh, wl, grad, rs_a, rs_b,
-    far_pan, far_own, fph, fpl, late_w, late_out, late_in,
+    far_pan, far_own, fph, fpl, late_w, late_c, late_out, late_in,
     local_sem, recv_sem, down_sem, up_sem, a_send, a_recv, b_send, b_recv,
-    fp_send, fp_recv, fo_send, fo_recv, ag_send, ag_recv, lw_send, lw_recv, lr_send, lr_recv,
+    misc_send, fp_recv, fo_recv, ag_recv, lw_recv, lc_recv, lr_recv,
 ):
     rows, rhs = res_ref.shape
     panels, width = diag_ref.shape[0], diag_ref.shape[1]
@@ -45,20 +45,25 @@
     tail = rows - width
     part = width // n_col
     chips = n_col // 2
-    piece = width // PIECES
+    offset = [sum(PIECES[:p]) for p in range(panels)]
     row, col = lax.axis_index("row"), lax.axis_index("col")
     core, chip = lax.rem(col, 2), col // 2
     last = panels - 1
     last_root = n_row - panels
     helper = last_root + 1
+    spared = row == last_root
+    lane = width // 2
+    lanes = 2 * blocks
+    late, corner = panels, panels + 1
 
     def columns(c):
         return pl.ds(pl.multiple_of(c * CHUNK, CHUNK), CHUNK)
 
     def y_copy(p, c, h, sems, step):
+        piece = width // PIECES[p]
         block = y.at[p, c, h * piece : (h + 1) * piece]
         return pltpu.make_async_remote_copy(
-            src_ref=block, dst_ref=block, send_sem=sems, recv_sem=recv_sem.at[p, c, h],
+            src_ref=block, dst_ref=block, send_sem=sems, recv_sem=recv_sem.at[c, offset[p] + h],
             device_id={"row": lax.rem(row + step, n_row)}, device_id_type=MESH,
         )
 
@@ -73,44 +78,50 @@
     def panel_part(n, step):
         return pltpu.make_async_remote_copy(
             src_ref=pan_hbm.at[:n, own_part, tail:], dst_ref=far_pan.at[:n, own_part],
-            send_sem=fp_send, recv_sem=fp_recv,
+            send_sem=misc_send, recv_sem=fp_recv,
             device_id={"row": lax.rem(row + step, n_row)}, device_id_type=MESH,
         )
 
     def panel_share(n, step):
         return pltpu.make_async_remote_copy(
             src_ref=far_pan.at[:n, own_part], dst_ref=far_pan.at[:n, own_part],
-            send_sem=ag_send, recv_sem=ag_recv,
+            send_sem=misc_send, recv_sem=ag_recv,
             device_id={"col": lax.rem(col + step, n_col)}, device_id_type=MESH,
         )
 
     def panel_shares(n):
         others = far_pan.at[:n, : (n_col - 1) * part]
         return pltpu.make_async_remote_copy(
-            src_ref=others, dst_ref=others, send_sem=ag_send, recv_sem=ag_recv,
+            src_ref=others, dst_ref=others, send_sem=misc_send, recv_sem=ag_recv,
             device_id={"col": lax.rem(col + 1, n_col)}, device_id_type=MESH,
         )
 
     def far_rows(c, step):
         return pltpu.make_async_remote_copy(
-            src_ref=cot_hbm.at[tail:, columns(c)], dst_ref=far_own.at[c], send_sem=fo_send, recv_sem=fo_recv.at[c],
+            src_ref=cot_hbm.at[tail:, columns(c)], dst_ref=far_own.at[c], send_sem=misc_send, recv_sem=fo_recv.at[c],
             device_id={"row": lax.rem(row + step, n_row)}, device_id_type=MESH,
         )
 
     def late_rows():
         return pltpu.make_async_remote_copy(
-            src_ref=wht_hbm.at[:, columns(LATE)], dst_ref=late_w, send_sem=lw_send, recv_sem=lw_recv,
+            src_ref=wht_hbm.at[:, columns(LATE)], dst_ref=late_w, send_sem=misc_send, recv_sem=lw_recv,
             device_id={"row": lax.rem(row + 1, n_row)}, device_id_type=MESH,
         )
 
+    def corner_rows():
+        return pltpu.make_async_remote_copy(
+            src_ref=wht_hbm.at[:lane], dst_ref=late_c, send_sem=misc_send, recv_sem=lc_recv,
+            device_id={"row": lax.rem(row + 1, n_row)}, device_id_type=MESH,
+        )
+
     def late_result():
         return pltpu.make_async_remote_copy(
-            src_ref=late_out, dst_ref=late_in, send_sem=lr_send, recv_sem=lr_recv,
+            src_ref=late_out, dst_ref=late_in, send_sem=misc_send, recv_sem=lr_recv,
             device_id={"row": lax.rem(row + n_row - 1, n_row)}, device_id_type=MESH,
         )
 
     def group(g):
-        return slice(0, blocks - 1) if g == 0 else slice(blocks - 1, blocks)
+        return (slice(0, lanes - 2), slice(1, 4), slice(4, lanes - 2), slice(lanes - 2, lanes))[g]
 
     def pair_copy(p, m, g):
         place = (2 * m + 1 - core) * part
@@ -144,38 +155,55 @@
 
     def y_all(p, first, sems, step):
         return pltpu.make_async_remote_copy(
-            src_ref=y.at[p, first:], dst_ref=y.at[p, first:], send_sem=sems, recv_sem=recv_sem.at[p, 0, 0],
+            src_ref=y.at[p, first:], dst_ref=y.at[p, first:], send_sem=sems, recv_sem=recv_sem.at[0, 0],
             device_id={"row": lax.rem(row + step, n_row)}, device_id_type=MESH,
         )
 
     def own_all():
         return pltpu.make_async_remote_copy(
-            src_ref=far_own, dst_ref=far_own, send_sem=fo_send, recv_sem=fo_recv.at[0],
+            src_ref=far_own, dst_ref=far_own, send_sem=misc_send, recv_sem=fo_recv.at[0],
             device_id={"row": lax.rem(row + 1, n_row)}, device_id_type=MESH,
         )
 
     def groups(p, act):
-        act(0)
-
-        @pl.when((row <= n_row - 1 - p) | (p >= panels))
+        if isinstance(p, int) and p >= panels:
+            for g in (1, 2, 3) if p == late else (3,):
+                act(g)
+            return
+
+        short = spared & (p >= last - 1)
+
+        @pl.when(jnp.logical_not(short))
+        def _():
+            act(0)
+
+        @pl.when(short)
         def _():
             act(1)
+            act(2)
+
+        @pl.when(row <= n_row - 1 - p)
+        def _():
+            act(3)
 
     def lower(p):
-        inner = lax.broadcasted_iota(jnp.int32, (width, width), 0)
-        within = lax.broadcasted_iota(jnp.int32, (width, width), 1)
-        grad[p, blocks - 1] = jnp.where(inner >= within, grad[p, blocks - 1], 0.0)
+        inner = lax.broadcasted_iota(jnp.int32, (width, lane), 0)
+        within = lax.broadcasted_iota(jnp.int32, (width, lane), 1)
+        for k in range(2):
+            at = lanes - 2 + k
+            grad[p, at] = jnp.where(inner >= within + k * lane, grad[p, at], 0.0)
+
+    def pair_group(p, g):
+        for m in range(chips):
+            pair_copy(p, m, g).start()
 
     def pair_start(p):
-        @pl.when(row == n_row - 1 - p)
-        def _():
-            lower(p)
-
-        def act(g):
-            for m in range(chips):
-                pair_copy(p, m, g).start()
-
-        groups(p, act)
+        if p < panels:
+            @pl.when(row == n_row - 1 - p)
+            def _():
+                lower(p)
+
+        groups(p, functools.partial(pair_group, p))
 
     def chip_start(p):
         def act(g):
@@ -197,8 +225,8 @@
     def finish(p):
         def act(g):
             chip_all(p, g).wait_recv()
-            for b in range(blocks)[group(g)]:
-                out_ref[p, :, b * width : (b + 1) * width] = total(p, b)
+            for b in range(lanes)[group(g)]:
+                out_ref[p, :, b * lane : (b + 1) * lane] = total(p, b)
 
         out_ref[p, :, tail:] = jnp.zeros((part, width), F32)
         groups(p, act)
@@ -207,15 +235,31 @@
         late_rows().wait_recv()
         yq = split(y[last, LATE])
         for b in range(blocks):
-            grad[panels, b] = -product(yq, split(late_w[b * width : (b + 1) * width]), NT)
-        lower(panels)
-        pair_start(panels)
+            value = product(yq, split(late_w[b * width : (b + 1) * width]), NT)
+            grad[late, 2 * b] = -value[:, :lane]
+            grad[late, 2 * b + 1] = -value[:, lane:]
+        lower(late)
+        pair_start(late)
+
+    def corner_work():
+        corner_rows().wait_recv()
+        for k in range(2):
+            value = None
+            for c in range(count):
+                term = product(split(y[last - 1 + k, c]), split(late_c[:, c * CHUNK : (c + 1) * CHUNK]), NT)
+                value = term if value is None else value + term
+            grad[corner, lanes - 2 + k] = -value
+        pair_start(corner)
 
     def late_finish():
-        for g in range(2):
-            chip_all(panels, g).wait_recv()
-        for b in range(blocks):
-            late_out[:, b * width : (b + 1) * width] = total(panels, b)
+        def act(p, shift, g):
+            chip_all(p, g).wait_recv()
+            for b in range(lanes)[group(g)]:
+                late_out[:, (b + shift) * lane : (b + shift + 1) * lane] = total(p, b)
+
+        late_out[:, :lane] = jnp.zeros((part, lane), F32)
+        groups(late, functools.partial(act, late, 0))
+        groups(corner, functools.partial(act, corner, 2))
         late_result().start()
 
     def solve(p, c, own):
@@ -235,7 +279,7 @@
             source = source | ((row == last_root) & ((c == RAW[0]) | (c == RAW[1])))
         if p == 1:
             source = source | (row == n_row - 1)
-        for h in range(PIECES):
+        for h in range(PIECES[p]):
             @pl.when(jnp.logical_not(source))
             def _():
                 y_copy(p, c, h, down_sem, n_row - 1).wait_recv()
@@ -249,7 +293,7 @@
                 down(p, c, h).start()
 
     def send(p, c, way):
-        for h in range(PIECES):
+        for h in range(PIECES[p]):
             way(p, c, h).start()
 
     def tail_update(p, c):
@@ -259,12 +303,25 @@
         @pl.when(row == n_row - 1 - p)
         def _():
             res_ref[tail:, columns(c)] = y[p, c]
+
+    def grad_block(q, c, yq, b):
+        at = slice(b * width, (b + 1) * width)
+        value = product(yq, (wh[c, at], wl[c, at]), NT)
+        grad[q, 2 * b] -= value[:, :lane]
+        grad[q, 2 * b + 1] -= value[:, lane:]
 
     def grad_work(q, c):
         yq = split(y[q, c])
         for b in range(blocks):
-            at = slice(b * width, (b + 1) * width)
-            grad[q, b] -= product(yq, (wh[c, at], wl[c, at]), NT)
+            grad_block(q, c, yq, b)
+
+    def grad_last(c):
+        yq = split(y[last - 1, c])
+        for b in range(blocks):
+            grad_block(last - 1, c, yq, b)
+            for g in range(1, 4):
+                if group(g).stop == 2 * b + 2:
+                    pair_group(last - 1, g)
 
     def res_work(q, c):
         yq = split(y[q, c])
@@ -332,10 +389,38 @@
     wht_copy = pltpu.make_async_copy(wht_hbm, wht_ref, local_sem.at[4])
     for copy in (diag_copy, tail_copy, pan_copy, wht_copy, head_copy):
         copy.start()
+    pl.semaphore_wait(barrier, 2 + n_col - 1)
+
+    @pl.when(row == helper)
+    def _():
+        panel_part(last - 1, n_row - 1).start()
+        for c in RAW:
+            far_rows(c, n_row - 1).start()
+
+    @pl.when(row == n_row - 2)
+    def _():
+        panel_part(1, 1).start()
+
+        @pl.loop(0, count)
+        def _(c):
+            far_rows(c, 1).start()
+
+    @pl.when(row == last_root)
+    def _():
+        panel_part(last, 1).start()
+        for c in range(LATE + 1):
+            far_rows(c, 1).start()
+        late_rows().start()
+
+        @pl.loop(LATE + 1, count)
+        def _(c):
+            far_rows(c, 1).start()
+
+        corner_rows().start()
+
     diag_copy.wait()
     inverse(0)
     tail_copy.wait()
-    pl.semaphore_wait(barrier, 2 + n_col - 1)
 
     @pl.when(row == n_row - 1)
     def _():
@@ -343,31 +428,6 @@
         def _(c):
             solve(0, c, res_ref[tail:, columns(c)])
             send(0, c, down)
-
-    @pl.when(row == helper)
-    def _():
-        panel_part(last - 1, n_row - 1).start()
-        for c in RAW:
-            far_rows(c, n_row - 1).start()
-
-    @pl.when(row == n_row - 2)
-    def _():
-        panel_part(1, 1).start()
-
-        @pl.loop(0, count)
-        def _(c):
-            far_rows(c, 1).start()
-
-    @pl.when(row == last_root)
-    def _():
-        panel_part(last, 1).start()
-        for c in range(LATE + 1):
-            far_rows(c, 1).start()
-        late_rows().start()
-
-        @pl.loop(LATE + 1, count)
-        def _(c):
-            far_rows(c, 1).start()
 
     @pl.loop(1, panels)
     def _(p):
@@ -408,8 +468,6 @@
     def _():
         take_panels(1)
 
-    spared = row == last_root
-
     @pl.when(row == helper)
     def _():
         take_panels(last)
@@ -457,9 +515,9 @@
             far(last, c)
             send(last, c, up)
 
-            @pl.when(c == count - 1)
-            def _():
-                chip_start(panels)
+            @pl.when(c == LATE + 1)
+            def _():
+                late_work()
 
         for q in range(1, last - 1):
             grad_work(q, c)
@@ -491,7 +549,7 @@
 
             @pl.when(c == LATE + 1)
             def _():
-                late_work()
+                chip_start(late)
 
     for p in range(1, last - 1):
         chip_start(p)
@@ -512,70 +570,81 @@
         def _():
             receive(last - 1, c)
 
-            @pl.when(t > bulk)
-            def _():
-                grad_work(last - 1, c)
+        @pl.when((row != helper) & jnp.logical_not(spared))
+        def _():
+            grad_work(last - 1, c)
+
+            @pl.when(t == count - 1)
+            def _():
                 pair_start(last - 1)
 
-            @pl.when(below)
-            def _():
-                tail_update(last - 1, c)
-
-                @pl.when(spared)
+        @pl.when(t > bulk)
+        def _():
+            grad_last(c)
+
+        @pl.when(below)
+        def _():
+            tail_update(last - 1, c)
+
+            @pl.when(spared)
+            def _():
+                solve(last, c, res_ref[tail:, columns(c)])
+
+                @pl.when(row > 0)
                 def _():
-                    solve(last, c, res_ref[tail:, columns(c)])
-
-                    @pl.when(row > 0)
-                    def _():
-                        send(last, c, down)
+                    send(last, c, down)
+
+        @pl.when(t > bulk)
+        def _():
+            chip_start(last - 1)
 
         keep(last - 1, c)
 
         @pl.when(row > helper)
         def _():
+            res_work(last - 1, c)
+
+            @pl.when((row == n_row - 1) & (t == count - 1))
+            def _():
+                chip_start(last - 1)
+
+        receive(last, c)
+
+        @pl.when(row < last_root)
+        def _():
+            tail_update(last, c)
+
+        keep(last, c)
+
+        @pl.when((row > helper) & (row < n_row - 1) & (t == count - 1) | (row == helper) & (t == 0))
+        def _():
+            chip_start(last - 1)
+
+        @pl.when(t <= bulk)
+        def _():
+            grad_work(last, c)
+
+            @pl.when(t == bulk)
+            def _():
+                pair_start(last)
+
+        @pl.when(spared & (t <= bulk))
+        def _():
             grad_work(last - 1, c)
 
-            @pl.when(t == count - 1)
-            def _():
-                pair_start(last - 1)
-
-            res_work(last - 1, c)
-
-            @pl.when((row == n_row - 1) & (t == count - 1))
-            def _():
-                chip_start(last - 1)
-
-        receive(last, c)
-
-        @pl.when(row < last_root)
-        def _():
-            tail_update(last, c)
-
-        keep(last, c)
-
-        @pl.when(((row >= helper) & (row < n_row - 1) & (t == count - 1)) | (t > bulk))
-        def _():
-            chip_start(last - 1)
-
-        @pl.when(t <= bulk)
-        def _():
-            grad_work(last, c)
-
             @pl.when(t == bulk)
             def _():
-                pair_start(last)
-
-        @pl.when(below & (t <= bulk))
-        def _():
-            grad_work(last - 1, c)
-
-            @pl.when(t == count - 1)
-            def _():
-                pair_start(last - 1)
-
-            @pl.when(spared & (t == bulk))
-            def _():
                 chip_start(last)
+
+        @pl.when(row == helper)
+        def _():
+            @pl.when(t == 1)
+            def _():
+                corner_work()
+
+            @pl.when(t == 2)
+            def _():
+                chip_start(corner)
 
         @pl.when(below)
         def _():
@@ -604,7 +673,9 @@
     @pl.when(spared)
     def _():
         late_result().wait_recv()
-        out_ref[last] += late_in[...]
+        out_ref[last - 1, :, :lane] = late_in[:, rows : rows + lane]
+        out_ref[last, :, lane:] += late_in[:, lane:rows]
+        out_ref[last, :, :lane] = late_in[:, rows + lane :]
 
 
     @pl.loop(0, panels)
@@ -633,9 +704,12 @@
             far_rows(c, n_row - 1).wait_send()
         panel_shares(last).wait_send()
         late_result().wait_send()
-        for g in range(2):
-            pair_all(panels, g).wait_send()
-            chip_all(panels, g).wait_send()
+        for p in (late, corner):
+            def act(g):
+                pair_all(p, g).wait_send()
+                chip_all(p, g).wait_send()
+
+            groups(p, act)
 
     @pl.when(row == n_row - 2)
     def _():
@@ -652,6 +726,7 @@
         own_all().wait_send()
         panel_shares(last - 1).wait_send()
         late_rows().wait_send()
+        corner_rows().wait_send()
 
 
 def store_kernel(res_ref, grad_ref, res_hbm, grad_hbm, sems):
@@ -672,7 +747,7 @@
     def body(cotangent, whitened, panel_rows, diag_inverse):
         rows, rhs = cotangent.shape
         panels, width = diag_inverse.shape[:2]
-        assert 3 <= panels <= n_row and n_col % 2 == 0 and rhs // CHUNK > RAW[1] + 1
+        assert panels == len(PIECES) <= n_row and n_col % 2 == 0 and rhs // CHUNK > RAW[1] + 1
         count, blocks, part, chips = rhs // CHUNK, rows // width, width // n_col, n_col // 2
         anywhere = pl.BlockSpec(memory_space=pl.ANY)
         vmem = pl.BlockSpec(memory_space=pltpu.VMEM)
@@ -694,30 +769,28 @@
                 pltpu.VMEM((panels, width, width), BF16),
                 pltpu.VMEM((count, rows, CHUNK), BF16),
                 pltpu.VMEM((count, rows, CHUNK), BF16),
-                pltpu.VMEM((panels + 1, blocks, width, width), F32),
-                pltpu.VMEM((panels + 1, chips, blocks, part, width), F32),
-                pltpu.VMEM((panels + 1, chips, blocks, part, width), F32),
+                pltpu.VMEM((panels + 2, 2 * blocks, width, width // 2), F32),
+                pltpu.VMEM((panels + 2, chips, 2 * blocks, part, width // 2), F32),
+                pltpu.VMEM((panels + 2, chips, 2 * blocks, part, width // 2), F32),
                 pltpu.VMEM((panels - 1, width, width), F32),
                 pltpu.VMEM((count, width, CHUNK), F32),
                 pltpu.VMEM((panels - 1, width, width), BF16),
                 pltpu.VMEM((panels - 1, width, width), BF16),
                 pltpu.VMEM((rows, CHUNK), F32),
-                pltpu.VMEM((part, rows), F32),
-                pltpu.VMEM((part, rows), F32),
+                pltpu.VMEM((width // 2, rhs), F32),
+                pltpu.VMEM((part, rows + width), F32),
+                pltpu.VMEM((part, rows + width), F32),
                 dma((5,)),
-                dma((panels, count, PIECES)),
-                dma,
-                dma,
-                dma,
-                dma((panels + 1, 2)),
-                dma,
-                dma((panels + 1, 2)),
-                dma,
+                dma((count, sum(PIECES))),
+                dma,
+                dma,
+                dma,
+                dma((panels + 2, 4)),
+                dma,
+                dma((panels + 2, 4)),
                 dma,
                 dma,
                 dma((count,)),
-                dma,
-                dma,
                 dma,
                 dma,
                 dma,

time: 89.9 us -> 88.4 us (0.983)
  Pallas kernels: 89 us -> 87.4 us
    pallas_call x1, Pallas kernels: 86.8 us -> 85.2 us  [body(): pl.pallas_call(functools.partial(kernel, n_row, n_col), out_shape=(pltpu....]
where the time goes in v4:
time: 88.4 us; the launch traced here: 88.2 us
  Pallas kernels  87.4 us (99%)
    pallas_call x1, Pallas kernels, body(): pl.pallas_call(functools.partial(kernel, n_row, n_col), out_shape=(pltpu....  85.2 us
    pallas_call x1, Pallas kernels, body(): pl.pallas_call(store_kernel, out_shape=tuple((jax.ShapeDtypeStruct(k.shap...  2.22 us

profile of v4, /device:TPU:0, one launch (start us, length us, event | category | flops | bytes accessed | tf_op | source)
XLA Modules:
  0.0 88.2 jit_solution(1537281263765485009)
XLA Ops:
  0.6 85.2 %shard_map.59 = (f32[1024,1024]{1,0:T(8,128)S(1)}, f32[4,32,1024]{2,1,0:T(8,128)S(1)}) custom-call(f32[1024,1024]{1,0:T(8,128)} %cot_hbm.1, f32[1024,1024]{1,0:T(8,128)} %wht_hbm.1, f32[4,256,1024]{2,1,0:T(8,128)} %pan_hbm.1, f32[4,256,256]{2,1,0:T(8,128)} %diag_hbm.1), custom_call_target="tpu_custom_call" | custom-call | tf_op jit(solution)/shard_map/pallas_call | solution.py:756
  85.8 2.2 %shard_map.60 = (f32[1024,1024]{1,0:T(8,128)}, f32[4,32,1024]{2,1,0:T(8,128)}) custom-call(f32[1024,1024]{1,0:T(8,128)S(1)} %get-tuple-element.4.res_ref, f32[4,32,1024]{2,1,0:T(8,128)S(1)} %get-tuple-element.5.grad_ref), custom_call_target="tpu_custom_call" | custom-call | tf_op jit(solution)/shard_map/pallas_call | solution.py:803

commit v5 on v4

--- a/solution.py
+++ b/solution.py
@@ -123,11 +123,16 @@
     def group(g):
         return (slice(0, lanes - 2), slice(1, 4), slice(4, lanes - 2), slice(lanes - 2, lanes))[g]
 
+    def slot(p, g):
+        if isinstance(p, int) and p >= panels:
+            return 3 * panels + (g - 1 if p == late else 3)
+        return 3 * p + (0, 0, 1, 2)[g]
+
     def pair_copy(p, m, g):
         place = (2 * m + 1 - core) * part
         return pltpu.make_async_remote_copy(
             src_ref=grad.at[p, group(g), pl.ds(pl.multiple_of(place, part), part)], dst_ref=rs_a.at[p, m, group(g)],
-            send_sem=a_send, recv_sem=a_recv.at[p, g],
+            send_sem=a_send, recv_sem=a_recv.at[slot(p, g)],
             device_id={"col": 2 * chip + 1 - core}, device_id_type=MESH,
         )
 
@@ -135,21 +140,21 @@
         peer = lax.rem(chip + j, chips)
         return pltpu.make_async_remote_copy(
             src_ref=rs_a.at[p, peer, group(g)], dst_ref=rs_b.at[p, j, group(g)],
-            send_sem=b_send, recv_sem=b_recv.at[p, g],
+            send_sem=b_send, recv_sem=b_recv.at[slot(p, g)],
             device_id={"col": 2 * peer + core}, device_id_type=MESH,
         )
 
     def pair_all(p, g):
         return pltpu.make_async_remote_copy(
             src_ref=rs_a.at[p, :, group(g)], dst_ref=rs_a.at[p, :, group(g)],
-            send_sem=a_send, recv_sem=a_recv.at[p, g],
+            send_sem=a_send, recv_sem=a_recv.at[slot(p, g)],
             device_id={"col": 2 * chip + 1 - core}, device_id_type=MESH,
         )
 
     def chip_all(p, g):
         return pltpu.make_async_remote_copy(
             src_ref=rs_b.at[p, 1:, group(g)], dst_ref=rs_b.at[p, 1:, group(g)],
-            send_sem=b_send, recv_sem=b_recv.at[p, g],
+            send_sem=b_send, recv_sem=b_recv.at[slot(p, g)],
             device_id={"col": 2 * lax.rem(chip + 1, chips) + core}, device_id_type=MESH,
         )
 
@@ -208,11 +213,12 @@
     def chip_start(p):
         def act(g):
             pair_all(p, g).wait_recv()
-            for m in range(chips):
+            for j in range(1, chips + 1):
+                m = lax.rem(chip + j, chips)
                 place = pl.multiple_of((2 * m + core) * part, part)
                 rs_a[p, m, group(g)] += grad[p, group(g), pl.ds(place, part)]
-            for j in range(1, chips):
-                chip_copy(p, j, g).start()
+                if j < chips:
+                    chip_copy(p, j, g).start()
 
         groups(p, act)
 
@@ -551,8 +557,10 @@
             def _():
                 chip_start(late)
 
-    for p in range(1, last - 1):
-        chip_start(p)
+    @pl.when(jnp.logical_not(passing))
+    def _():
+        for p in range(1, last - 1):
+            chip_start(p)
 
     @pl.when(row == helper)
     def _():
@@ -610,6 +618,11 @@
 
         receive(last, c)
 
+        @pl.when(passing & (t == 0))
+        def _():
+            for p in range(1, last - 1):
+                chip_start(p)
+
         @pl.when(row < last_root)
         def _():
             tail_update(last, c)
@@ -666,27 +679,11 @@
     @pl.when(row == helper)
     def _():
         late_finish()
-
-    finish(last)
-    finish(last - 1)
-
-    @pl.when(spared)
-    def _():
-        late_result().wait_recv()
-        out_ref[last - 1, :, :lane] = late_in[:, rows : rows + lane]
-        out_ref[last, :, lane:] += late_in[:, lane:rows]
-        out_ref[last, :, :lane] = late_in[:, rows + lane :]
-
 
     @pl.loop(0, panels)
     def _(p):
         root = n_row - 1 - p
-
-        def act(g):
-            pair_all(p, g).wait_send()
-            chip_all(p, g).wait_send()
-
-        groups(p, act)
+        groups(p, lambda g: pair_all(p, g).wait_send())
 
         @pl.when((row >= root) & (row < n_row - 1) & ((p < last) | (row > last_root)) & (p != 1))
         def _():
@@ -703,13 +700,9 @@
         for c in RAW:
             far_rows(c, n_row - 1).wait_send()
         panel_shares(last).wait_send()
-        late_result().wait_send()
         for p in (late, corner):
-            def act(g):
-                pair_all(p, g).wait_send()
-                chip_all(p, g).wait_send()
-
-            groups(p, act)
+            groups(p, lambda g: pair_all(p, g).wait_send())
+            groups(p, lambda g: chip_all(p, g).wait_send())
 
     @pl.when(row == n_row - 2)
     def _():
@@ -727,6 +720,26 @@
         panel_shares(last - 1).wait_send()
         late_rows().wait_send()
         corner_rows().wait_send()
+
+    for p in range(last - 1):
+        groups(p, lambda g: chip_all(p, g).wait_send())
+
+    finish(last)
+    finish(last - 1)
+
+    @pl.when(spared)
+    def _():
+        late_result().wait_recv()
+        out_ref[last - 1, :, :lane] = late_in[:, rows : rows + lane]
+        out_ref[last, :, lane:] += late_in[:, lane:rows]
+        out_ref[last, :, :lane] = late_in[:, rows + lane :]
+
+    for p in (last - 1, last):
+        groups(p, lambda g: chip_all(p, g).wait_send())
+
+    @pl.when(row == helper)
+    def _():
+        late_result().wait_send()
 
 
 def store_kernel(res_ref, grad_ref, res_hbm, grad_hbm, sems):
@@ -785,9 +798,9 @@
                 dma,
                 dma,
                 dma,
-                dma((panels + 2, 4)),
-                dma,
-                dma((panels + 2, 4)),
+                dma((3 * panels + 4,)),
+                dma,
+                dma((3 * panels + 4,)),
                 dma,
                 dma,
                 dma((count,)),

time: 88.4 us -> 88.1 us (level)
  no operation moved by 1% of the time
where the time goes in v5:
time: 88.1 us; the launch traced here: 88 us
  Pallas kernels  87.2 us (99%)
    pallas_call x1, Pallas kernels, body(): pl.pallas_call(functools.partial(kernel, n_row, n_col), out_shape=(pltpu....  85 us
    pallas_call x1, Pallas kernels, body(): pl.pallas_call(store_kernel, out_shape=tuple((jax.ShapeDtypeStruct(k.shap...  2.22 us

profile of v5, /device:TPU:0, one launch (start us, length us, event | category | flops | bytes accessed | tf_op | source)
XLA Modules:
  0.0 88.0 jit_solution(17155171772122769251)
XLA Ops:
  0.6 85.0 %shard_map.59 = (f32[1024,1024]{1,0:T(8,128)S(1)}, f32[4,32,1024]{2,1,0:T(8,128)S(1)}) custom-call(f32[1024,1024]{1,0:T(8,128)} %cot_hbm.1, f32[1024,1024]{1,0:T(8,128)} %wht_hbm.1, f32[4,256,1024]{2,1,0:T(8,128)} %pan_hbm.1, f32[4,256,256]{2,1,0:T(8,128)} %diag_hbm.1), custom_call_target="tpu_custom_call" | custom-call | tf_op jit(solution)/shard_map/pallas_call | solution.py:769
  85.6 2.2 %shard_map.60 = (f32[1024,1024]{1,0:T(8,128)}, f32[4,32,1024]{2,1,0:T(8,128)}) custom-call(f32[1024,1024]{1,0:T(8,128)S(1)} %get-tuple-element.4.res_ref, f32[4,32,1024]{2,1,0:T(8,128)S(1)} %get-tuple-element.5.grad_ref), custom_call_target="tpu_custom_call" | custom-call | tf_op jit(solution)/shard_map/pallas_call | solution.py:816

commit v6 on v5

--- a/solution.py
+++ b/solution.py
@@ -9,7 +9,7 @@
 
 MESH = pl.DeviceIdType.MESH
 CHUNK = 256
-PIECES = (4, 4, 2, 4)
+PIECES = (4, 4, 1, 2)
 STORES = 4
 RAW = (0, 2)
 LATE = 1
@@ -321,13 +321,15 @@
         for b in range(blocks):
             grad_block(q, c, yq, b)
 
-    def grad_last(c):
-        yq = split(y[last - 1, c])
+    def grad_last(q, c):
+        yq = split(y[q, c])
         for b in range(blocks):
-            grad_block(last - 1, c, yq, b)
+            grad_block(q, c, yq, b)
+            if q == last and b == blocks - 1:
+                lower(q)
             for g in range(1, 4):
                 if group(g).stop == 2 * b + 2:
-                    pair_group(last - 1, g)
+                    pair_group(q, g)
 
     def res_work(q, c):
         yq = split(y[q, c])
@@ -588,7 +590,7 @@
 
         @pl.when(t > bulk)
         def _():
-            grad_last(c)
+            grad_last(last - 1, c)
 
         @pl.when(below)
         def _():
@@ -633,7 +635,7 @@
         def _():
             chip_start(last - 1)
 
-        @pl.when(t <= bulk)
+        @pl.when((t < bulk) | jnp.logical_not(spared))
         def _():
             grad_work(last, c)
 
@@ -641,13 +643,14 @@
             def _():
                 pair_start(last)
 
+        @pl.when(spared & (t == bulk))
+        def _():
+            grad_last(last, c)
+            chip_start(last)
+
         @pl.when(spared & (t <= bulk))
         def _():
             grad_work(last - 1, c)
-
-            @pl.when(t == bulk)
-            def _():
-                chip_start(last)
 
         @pl.when(row == helper)
         def _():

time: 88.1 us -> 88 us (level)
  no operation moved by 1% of the time
where the time goes in v6:
time: 88 us; the launch traced here: 87.8 us
  Pallas kernels  87 us (99%)
    pallas_call x1, Pallas kernels, body(): pl.pallas_call(functools.partial(kernel, n_row, n_col), out_shape=(pltpu....  84.8 us
    pallas_call x1, Pallas kernels, body(): pl.pallas_call(store_kernel, out_shape=tuple((jax.ShapeDtypeStruct(k.shap...  2.22 us

profile of v6, /device:TPU:0, one launch (start us, length us, event | category | flops | bytes accessed | tf_op | source)
XLA Modules:
  0.0 87.8 jit_solution(9414714665072165767)
XLA Ops:
  0.6 84.8 %shard_map.59 = (f32[1024,1024]{1,0:T(8,128)S(1)}, f32[4,32,1024]{2,1,0:T(8,128)S(1)}) custom-call(f32[1024,1024]{1,0:T(8,128)} %cot_hbm.1, f32[1024,1024]{1,0:T(8,128)} %wht_hbm.1, f32[4,256,1024]{2,1,0:T(8,128)} %pan_hbm.1, f32[4,256,256]{2,1,0:T(8,128)} %diag_hbm.1), custom_call_target="tpu_custom_call" | custom-call | tf_op jit(solution)/shard_map/pallas_call | solution.py:772
  85.5 2.2 %shard_map.60 = (f32[1024,1024]{1,0:T(8,128)}, f32[4,32,1024]{2,1,0:T(8,128)}) custom-call(f32[1024,1024]{1,0:T(8,128)S(1)} %get-tuple-element.4.res_ref, f32[4,32,1024]{2,1,0:T(8,128)S(1)} %get-tuple-element.5.grad_ref), custom_call_target="tpu_custom_call" | custom-call | tf_op jit(solution)/shard_map/pallas_call | solution.py:819

commit v7 on v6

--- a/solution.py
+++ b/solution.py
@@ -10,7 +10,7 @@
 MESH = pl.DeviceIdType.MESH
 CHUNK = 256
 PIECES = (4, 4, 1, 2)
-STORES = 4
+STORES = 1
 RAW = (0, 2)
 LATE = 1
 F32 = jnp.float32
@@ -728,7 +728,6 @@
         groups(p, lambda g: chip_all(p, g).wait_send())
 
     finish(last)
-    finish(last - 1)
 
     @pl.when(spared)
     def _():
@@ -736,6 +735,8 @@
         out_ref[last - 1, :, :lane] = late_in[:, rows : rows + lane]
         out_ref[last, :, lane:] += late_in[:, lane:rows]
         out_ref[last, :, :lane] = late_in[:, rows + lane :]
+
+    finish(last - 1)
 
     for p in (last - 1, last):
         groups(p, lambda g: chip_all(p, g).wait_send())

time: 88 us -> 88 us (level)
  no operation moved by 1% of the time
where the time goes in v7:
time: 88 us; the launch traced here: 87.8 us
  Pallas kernels  87 us (99%)
    pallas_call x1, Pallas kernels, body(): pl.pallas_call(functools.partial(kernel, n_row, n_col), out_shape=(pltpu....  84.8 us
    pallas_call x1, Pallas kernels, body(): pl.pallas_call(store_kernel, out_shape=tuple((jax.ShapeDtypeStruct(k.shap...  2.2 us

profile of v7, /device:TPU:0, one launch (start us, length us, event | category | flops | bytes accessed | tf_op | source)
XLA Modules:
  0.0 87.8 jit_solution(17612195794710278544)
XLA Ops:
  0.6 84.8 %shard_map.59 = (f32[1024,1024]{1,0:T(8,128)S(1)}, f32[4,32,1024]{2,1,0:T(8,128)S(1)}) custom-call(f32[1024,1024]{1,0:T(8,128)} %cot_hbm.1, f32[1024,1024]{1,0:T(8,128)} %wht_hbm.1, f32[4,256,1024]{2,1,0:T(8,128)} %pan_hbm.1, f32[4,256,256]{2,1,0:T(8,128)} %diag_hbm.1), custom_call_target="tpu_custom_call" | custom-call | tf_op jit(solution)/shard_map/pallas_call | solution.py:773
  85.4 2.2 %shard_map.60 = (f32[1024,1024]{1,0:T(8,128)}, f32[4,32,1024]{2,1,0:T(8,128)}) custom-call(f32[1024,1024]{1,0:T(8,128)S(1)} %get-tuple-element.4.res_ref, f32[4,32,1024]{2,1,0:T(8,128)S(1)} %get-tuple-element.5.grad_ref), custom_call_target="tpu_custom_call" | custom-call | tf_op jit(solution)/shard_map/pallas_call | solution.py:820
